TPU v7x, 128 devices: a whole 4x4x4 slice. The times are simulated.
128 devices in a mesh: seq: 8 (over z_lo, x), exp: 16 (over z_hi, y, core).
Axes of the slice: x: 4, y: 4, z: 4 (z_hi: 2, z_lo: 2; z = z_hi * 2 + z_lo), core: 2. Of those that a mesh axis runs over, the one named last changes fastest.
Arguments:
- tokens: bfloat16 [2, 98304, 1024], P(None, ('seq', 'exp')), may hold values from -60 to 60
- router: bfloat16 [1024, 128], replicated, may hold values from -0.25 to 0.25
- w_in: bfloat16 [32, 1024, 4096], P('exp', None, 'seq'), may hold values from -0.1875 to 0.1875
- w_out: bfloat16 [32, 4096, 1024], P('exp', 'seq'), may hold values from -0.09375 to 0.09375
- grad_out: bfloat16 [2, 98304, 1024], P(None, ('seq', 'exp')), may hold values from -6 to 6
Outputs:
- mixed: bfloat16 [2, 98304, 1024], P(None, ('seq', 'exp'))
- grad_tokens: bfloat16 [2, 98304, 1024], P(None, ('seq', 'exp'))
- grad_router: float32 [1024, 128], P(('seq', 'exp'))
- grad_w_in: bfloat16 [32, 1024, 4096], P('exp', None, 'seq')
- grad_w_out: bfloat16 [32, 4096, 1024], P('exp', 'seq')
All inputs are finite; a program needn't handle non-finite values.
Results may differ from a plain program's by a relative error of at most 0.018.
Values may be sent and summed in bfloat16 or wider, within the bound.
No kernel may reach another device: no remote copies, remote signals or barrier semaphores. Data moves between devices by JAX's collectives and lax.ppermute only.
A program may use at most 128 MiB of HBM per device.

v0:
```python
import functools

import jax
import jax.numpy as jnp
from jax import lax
from jax.sharding import Mesh
from jax.sharding import PartitionSpec as P

EXP = ("exp_0", "exp_1", "exp_2")
SEQ_EXP = ("seq_0", "seq_1", "exp_0", "exp_1", "exp_2")
SEQ = ("seq_0", "seq_1")


def gathered_once(array, axis):
    leaves = jax.tree.leaves(array)
    turns = sorted(range(len(leaves)), key=lambda k: -leaves[k].size)
    width = (1, *leaves[turns[0]].shape)[-1]
    lines = [
        jnp.pad(leaves[k].reshape(-1), (0, -leaves[k].size % width)).reshape(-1, width)
        for k in turns
    ]
    both, at, found = (lax.all_gather(jnp.concatenate(lines), axis), 0, {})
    for k, line in zip(turns, lines):
        section = both[:, at : at + len(line)].reshape(len(both), -1)
        found[k] = section[:, : leaves[k].size].reshape(-1, *leaves[k].shape)
        at += len(line)
    numbers = iter(range(len(leaves)))
    return jax.tree.map(lambda _: found[next(numbers)], array)


def merged_by_axis(array, axes, combine):
    for axis in axes:
        pieces = gathered_once(array, axis)
        array = jax.tree.map(lambda part: part[0], pieces)
        for k in range(1, lax.axis_size(axis)):
            array = combine(array, jax.tree.map(lambda part: part[k], pieces))
    return array


def split_up(array, dim, peers):
    before, after = (array.shape[:dim], array.shape[dim + 1 :])
    return jnp.moveaxis(array.reshape(*before, peers, -1, *after), dim, 0)


def sent_and_summed(array, axis, dim):
    parts = split_up(array, dim, lax.axis_size(axis))
    arrived = lax.all_to_all(parts, axis, split_axis=0, concat_axis=0, tiled=True)
    return arrived.sum(axis=0)


def from_everyone(array, axis):
    copies = jnp.broadcast_to(array, (lax.axis_size(axis), *array.shape))
    return lax.all_to_all(copies, axis, split_axis=0, concat_axis=0, tiled=True)


def over_copies(array, axis):
    return from_everyone(array, axis).sum(axis=0)


def over_copies_2(array, axis):
    return from_everyone(array, axis).astype(jnp.float32).sum(axis=0)


def laid_out(parts, dim):
    shape = list(parts.shape[1:])
    shape[dim] *= parts.shape[0]
    return jnp.moveaxis(parts, 0, dim).reshape(shape)


def gather_directly(array, axis, dim):
    parts = from_everyone(array, axis)
    return laid_out(parts, dim)


def by_axis(array, axes):
    return functools.reduce(lax.psum, axes, array)


def merge_stats(first, second):
    top_value = jnp.maximum(first[0], second[0])
    return (
        top_value,
        first[1] * jnp.exp(first[0] - top_value) + second[1] * jnp.exp(second[0] - top_value),
    )


def on_device(tokens, router, w_in, w_out, grad_out):
    clips, tok_rows, width = tokens.shape
    slot_total = router.shape[1]
    owned = slot_total // lax.axis_size(EXP)
    experts_here = w_in.shape[0]
    per_expert = owned // experts_here
    logits = jnp.dot(
        tokens.reshape(clips * tok_rows, width), router, preferred_element_type=jnp.float32
    ).reshape(clips, tok_rows, slot_total)
    local_peak = jnp.max(logits, axis=1)
    local_mass = jnp.sum(jnp.exp(logits - local_peak[:, None, :]), axis=1)
    slot_peak, slot_mass = merged_by_axis((local_peak, local_mass), SEQ_EXP, merge_stats)
    exp_terms = jnp.exp(logits - slot_peak[:, None, :])
    dispatch = exp_terms / slot_mass[:, None, :]
    dispatch_b = dispatch.astype(jnp.bfloat16)
    mixing = jax.nn.softmax(logits, axis=2)
    mixing_b = mixing.astype(jnp.bfloat16)
    inputs = jnp.einsum("cts,ctd->scd", dispatch_b, tokens, preferred_element_type=jnp.float32)
    grads = jnp.einsum("cts,ctd->scd", mixing_b, grad_out, preferred_element_type=jnp.float32)
    column_sums = sent_and_summed(jnp.concatenate([inputs, grads], axis=1), EXP, 0)
    owner_sums = over_copies(column_sums, SEQ)
    expert_rows = (
        owner_sums[:, :clips].astype(jnp.bfloat16).reshape(experts_here, per_expert * clips, width)
    )
    grad_rows = (
        owner_sums[:, clips:].astype(jnp.bfloat16).reshape(experts_here, per_expert * clips, width)
    )
    pre = jnp.einsum("erd,edh->erh", expert_rows, w_in, preferred_element_type=jnp.float32)
    hidden = jax.nn.gelu(pre).astype(jnp.bfloat16)
    expert_part = jnp.einsum("erh,ehd->erd", hidden, w_out, preferred_element_type=jnp.float32)
    hidden_grad = jnp.einsum("erd,ehd->erh", grad_rows, w_out, preferred_element_type=jnp.float32)
    pre_grad = jax.vjp(jax.nn.gelu, pre)[1](hidden_grad)[0].astype(jnp.bfloat16)
    grad_w_out = jnp.einsum(
        "erh,erd->ehd", hidden, grad_rows, preferred_element_type=jnp.float32
    ).astype(jnp.bfloat16)
    grad_w_in = jnp.einsum(
        "erd,erh->edh", expert_rows, pre_grad, preferred_element_type=jnp.float32
    ).astype(jnp.bfloat16)
    input_part = jnp.einsum("erh,edh->erd", pre_grad, w_in, preferred_element_type=jnp.float32)
    out_sums, in_sums = (
        over_copies_2(expert_part.astype(jnp.bfloat16), SEQ).astype(jnp.float32),
        over_copies_2(input_part.astype(jnp.bfloat16), SEQ).astype(jnp.float32),
    )
    slot_outputs = out_sums.astype(jnp.bfloat16).reshape(owned, clips, width)
    slot_in_grads = in_sums.astype(jnp.bfloat16).reshape(owned, clips, width)
    shard_rows = gather_directly(slot_outputs, EXP, 0)
    weights = mixing_b
    outputs = jnp.einsum("cts,scd->ctd", weights, shard_rows, preferred_element_type=jnp.float32)
    block = jnp.einsum("ctd,scd->cts", grad_out, shard_rows, preferred_element_type=jnp.float32)
    mixed = outputs
    mixing_grad = block
    shard_rows = gather_directly(slot_in_grads, EXP, 0)
    weights = dispatch_b
    outputs = jnp.einsum("cts,scd->ctd", weights, shard_rows, preferred_element_type=jnp.float32)
    block = jnp.einsum("ctd,scd->cts", tokens, shard_rows, preferred_element_type=jnp.float32)
    inner = by_axis(jnp.sum(dispatch * block, axis=1), SEQ_EXP)
    logit_grad = dispatch * (block - inner[:, None, :]) + mixing * (
        mixing_grad - jnp.sum(mixing * mixing_grad, axis=2, keepdims=True)
    )
    logit_b = logit_grad.astype(jnp.bfloat16)
    router_part = jnp.dot(
        logit_b.reshape(clips * tok_rows, slot_total), router.T, preferred_element_type=jnp.float32
    ).reshape(clips, tok_rows, width)
    grad_tokens = (outputs + router_part).astype(jnp.bfloat16)
    grad_router = lax.psum_scatter(
        jnp.einsum("ctd,cts->ds", tokens, logit_b, preferred_element_type=jnp.float32),
        SEQ_EXP,
        scatter_dimension=0,
        tiled=True,
    )
    return (mixed.astype(jnp.bfloat16), grad_tokens, grad_router, grad_w_in, grad_w_out)


def solution(mesh):
    finer = Mesh(mesh.devices.reshape(2, 4, 2, 4, 2), ("seq_0", "seq_1", "exp_0", "exp_1", "exp_2"))
    return jax.shard_map(
        on_device,
        mesh=finer,
        in_specs=(
            P(None, SEQ_EXP, None),
            P(),
            P(EXP, None, SEQ),
            P(EXP, SEQ, None),
            P(None, SEQ_EXP, None),
        ),
        out_specs=(
            P(None, SEQ_EXP, None),
            P(None, SEQ_EXP, None),
            P(SEQ_EXP, None),
            P(EXP, None, SEQ),
            P(EXP, SEQ, None),
        ),
        check_vma=False,
    )
```

profile of v0, /device:TPU:1, one launch (start us, length us, event | category | flops | bytes accessed | tf_op | source)
XLA Modules:
  0.0 371.8 jit_solution(220535439359990274)
XLA Ops:
  12.3 4.2 %all-gather.5 = f32[2,4,128]{2,1,0:T(4,128)S(1)} all-gather(f32[1,4,128]{2,1,0:T(4,128)S(1)} %maximum_bitcast_fusion.1), channel_id=2, replica_groups=mesh['seq_0'=2,'seq_1'=4,'exp_0'=2,'exp_1'=4,'exp_2'=2] {'seq_0'}, dimensions={0}, use_global_device_ids=true | all-gather | bytes 6144 | tf_op jit(solution)/shard_map/all_gather | solution.py:22
  16.5 8.4 %all-gather.6 = f32[4,4,128]{2,1,0:T(4,128)S(1)} all-gather(f32[1,4,128]{2,1,0:T(4,128)S(1)} %maximum_bitcast_fusion.2), channel_id=3, replica_groups=mesh['seq_0'=2,'seq_1'=4,'exp_0'=2,'exp_1'=4,'exp_2'=2] {'seq_1'}, dimensions={0}, use_global_device_ids=true | all-gather | bytes 10240 | tf_op jit(solution)/shard_map/all_gather | solution.py:22
  25.0 5.1 %all-gather.7 = f32[2,4,128]{2,1,0:T(4,128)S(1)} all-gather(f32[1,4,128]{2,1,0:T(4,128)S(1)} %maximum_bitcast_fusion.3), channel_id=4, replica_groups=mesh['seq_0'=2,'seq_1'=4,'exp_0'=2,'exp_1'=4,'exp_2'=2] {'exp_0'}, dimensions={0}, use_global_device_ids=true | all-gather | bytes 6144 | tf_op jit(solution)/shard_map/all_gather | solution.py:22
  30.2 8.6 %all-gather.8 = f32[4,4,128]{2,1,0:T(4,128)S(1)} all-gather(f32[1,4,128]{2,1,0:T(4,128)S(1)} %maximum_bitcast_fusion.4), channel_id=5, replica_groups=mesh['seq_0'=2,'seq_1'=4,'exp_0'=2,'exp_1'=4,'exp_2'=2] {'exp_1'}, dimensions={0}, use_global_device_ids=true | all-gather | bytes 10240 | tf_op jit(solution)/shard_map/all_gather | solution.py:22
  38.8 9.5 %all-gather.9 = f32[2,4,128]{2,1,0:T(4,128)S(1)} all-gather(f32[1,4,128]{2,1,0:T(4,128)S(1)} %maximum_bitcast_fusion.5), channel_id=6, replica_groups=mesh['seq_0'=2,'seq_1'=4,'exp_0'=2,'exp_1'=4,'exp_2'=2] {'exp_2'}, dimensions={0}, use_global_device_ids=true | all-gather | bytes 6144 | tf_op jit(solution)/shard_map/all_gather | solution.py:22
  50.5 6.4 %convolution_bitcast_fusion = f32[128,2,1024]{2,0,1:T(8,128)} fusion(bf16[2,768,1024]{2,1,0:T(8,128)(2,1)} %param.9, f32[2,768]{1,0:T(2,128)S(1)} %get-tuple-element.37, f32[2,768,128]{2,1,0:T(8,128)} %copy-done.1), kind=kOutput, calls=%fused_computation.8 | convolution fusion | flops 403244672 | bytes 4986880 | tf_op jit(solution)/shard_map/cts,ctd->scd/dot_general | solution.py:105
  58.8 34.8 %all_to_all.30 = f32[16,8,4,1024]{3,1,2,0:T(8,128)} all-to-all(f32[16,8,4,1024]{3,1,2,0:T(8,128)S(1)} %copy.39), channel_id=1, replica_groups=mesh['seq_0'=2,'seq_1'=4,'exp_0'=2,'exp_1'=4,'exp_2'=2] {'exp_0','exp_1'..., dimensions={0} | all-to-all | bytes 4194304 | tf_op jit(solution)/shard_map/all_to_all | solution.py:47
  95.4 17.9 %all_to_all.31 = f32[8,8,4,1024]{3,1,2,0:T(8,128)} all-to-all(f32[8,8,4,1024]{3,1,2,0:T(8,128)S(1)} %broadcast_in_dim.10), channel_id=1, replica_groups=mesh['seq_0'=2,'seq_1'=4,'exp_0'=2,'exp_1'=4,'exp_2'=2] {'seq_0','seq_1'}, dimensions={0} | all-to-all | bytes 2097152 | tf_op jit(solution)/shard_map/all_to_all | solution.py:53
  125.9 4.2 %all-to-all-done.4 = bf16[8,2,8,1024]{3,2,1,0:T(8,128)(2,1)S(1)} async-done(((bf16[8,2,8,1024]{3,2,1,0:T(8,128)(2,1)}), bf16[8,2,8,1024]{3,2,1,0:T(8,128)(2,1)S(1)}, u32[]{:S(2)}, u32[]{:S(2)}) %all-to-all-start.4) | async-done | bytes 262176 | tf_op jit(solution)/shard_map/all_to_all | solution.py:53
  136.8 3.7 all-to-all-done.2
  141.3 8.3 %all-to-all-start.5 = ((bf16[16,8,2,1024]{3,1,2,0:T(8,128)(2,1)}), bf16[16,8,2,1024]{3,1,2,0:T(8,128)(2,1)}, u32[]{:S(2)}, u32[]{:S(2)}) async-start(bf16[16,8,2,1024]{3,1,2,0:T(8,128)(2,1)} %broadcast_in_dim.26), calls=%async_computation.5 | async-start | bytes 1048576 | tf_op jit(solution)/shard_map/all_to_all | solution.py:53
  151.8 9.4 %all-to-all-done.5 = bf16[16,8,2,1024]{3,1,2,0:T(8,128)(2,1)} async-done(((bf16[16,8,2,1024]{3,1,2,0:T(8,128)(2,1)}), bf16[16,8,2,1024]{3,1,2,0:T(8,128)(2,1)}, u32[]{:S(2)}, u32[]{:S(2)}) %all-to-all-start.5) | async-done | bytes 524320 | tf_op jit(solution)/shard_map/all_to_all | solution.py:53
  162.1 5.0 %all-to-all-start.3 = ((bf16[16,8,2,1024]{3,1,2,0:T(8,128)(2,1)}), bf16[16,8,2,1024]{3,1,2,0:T(8,128)(2,1)}, u32[]{:S(2)}, u32[]{:S(2)}) async-start(bf16[16,8,2,1024]{3,1,2,0:T(8,128)(2,1)} %broadcast_in_dim.24), calls=%async_computation.3 | async-start | bytes 1048576 | tf_op jit(solution)/shard_map/all_to_all | solution.py:53
  172.4 4.3 %psum.35 = f32[2,128]{1,0:T(2,128)S(1)} all-reduce(f32[2,128]{1,0:T(2,128)S(1)} %get-tuple-element.43), channel_id=1, replica_groups=mesh['seq_0'=2,'seq_1'=4,'exp_0'=2,'exp_1'=4,'exp_2'=2] {'seq_0'}, use_global_device_ids=true, to_apply=%region_9.10 | all-reduce | flops 256 | bytes 2048 | tf_op jit(solution)/shard_map/psum | solution.py:76
  176.7 6.8 %psum.36 = f32[2,128]{1,0:T(2,128)S(1)} all-reduce(f32[2,128]{1,0:T(2,128)S(1)} %psum.35), channel_id=1, replica_groups=mesh['seq_0'=2,'seq_1'=4,'exp_0'=2,'exp_1'=4,'exp_2'=2] {'seq_1'}, use_global_device_ids=true, to_apply=%region_10.11 | all-reduce | flops 256 | bytes 2048 | tf_op jit(solution)/shard_map/psum | solution.py:76
  183.5 5.3 %psum.37 = f32[2,128]{1,0:T(2,128)S(1)} all-reduce(f32[2,128]{1,0:T(2,128)S(1)} %psum.36), channel_id=1, replica_groups=mesh['seq_0'=2,'seq_1'=4,'exp_0'=2,'exp_1'=4,'exp_2'=2] {'exp_0'}, use_global_device_ids=true, to_apply=%region_11.12 | all-reduce | flops 256 | bytes 2048 | tf_op jit(solution)/shard_map/psum | solution.py:76
  188.8 8.6 %psum.38 = f32[2,128]{1,0:T(2,128)S(1)} all-reduce(f32[2,128]{1,0:T(2,128)S(1)} %psum.37), channel_id=1, replica_groups=mesh['seq_0'=2,'seq_1'=4,'exp_0'=2,'exp_1'=4,'exp_2'=2] {'exp_1'}, use_global_device_ids=true, to_apply=%region_12.13 | all-reduce | flops 256 | bytes 2048 | tf_op jit(solution)/shard_map/psum | solution.py:76
  197.4 8.5 %psum.39 = f32[2,128]{1,0:T(2,128)S(1)} all-reduce(f32[2,128]{1,0:T(2,128)S(1)} %psum.38), channel_id=1, replica_groups=mesh['seq_0'=2,'seq_1'=4,'exp_0'=2,'exp_1'=4,'exp_2'=2] {'exp_2'}, use_global_device_ids=true, to_apply=%region_13.14 | all-reduce | flops 256 | bytes 2048 | tf_op jit(solution)/shard_map/psum | solution.py:76
  206.0 3.9 %convolution_bitcast_fusion.2 = f32[2,768,128]{2,1,0:T(8,128)} fusion(bf16[2,768,1024]{2,1,0:T(8,128)(2,1)} %param.9, bf16[16,8,2,1024]{3,1,2,0:T(8,128)(2,1)} %all-to-all-done.3), kind=kOutput, calls=%fused_computation.11 | convolution fusion | flops 402653184 | bytes 4456448 | tf_op jit(solution)/shard_map/ctd,scd->cts/dot_general | solution.py:135
  209.9 11.4 %convolution_bitcast_fusion.4 = f32[1024,128]{0,1:T(8,128)} fusion(bf16[2,768,1024]{2,1,0:T(8,128)(2,1)S(1)} %copy-done, f32[2,768,128]{2,1,0:T(8,128)} %convolution_bitcast_fusion.2, f32[2,768,128]{2,1,0:T(8,128)} %get-tuple-element.44, f32[2,128]{1,0:T(2,128)S(1)} %psum.39, f32[2,768,128]{2,1,0:T(8,128)} %get-tuple-element.38, ...), kind=kOutput, calls=%fused_computation.17 | convolution fusion | flops 404817536 | bytes 6824960 | tf_op jit(solution)/shard_map/ctd,cts->ds/dot_general | solution.py:152
  221.4 5.0 %fusion.13 = f32[2,768,1024]{2,1,0:T(8,128)} fusion(bf16[16,8,2,1024]{3,1,2,0:T(8,128)(2,1)} %all-to-all-done.5, f32[2,768,128]{2,1,0:T(8,128)} %copy-done.1, f32[2,128]{1,0:T(2,128)S(1)} %copy-done.6, f32[2,128]{1,0:T(2,128)S(1)} %copy-done.8), kind=kOutput, calls=%fused_computation.28 | convolution fusion | flops 403243008 | bytes 7604224 | tf_op jit(solution)/shard_map/cts,scd->ctd/dot_general | solution.py:140
  226.3 13.7 %add_convert_fusion = bf16[2,768,1024]{2,1,0:T(8,128)(2,1)} fusion(f32[2,768,1024]{2,1,0:T(8,128)} %fusion.13, f32[2,768,128]{2,1,0:T(8,128)} %convolution_bitcast_fusion.2, f32[2,768,128]{2,1,0:T(8,128)} %get-tuple-element.44, f32[2,128]{1,0:T(2,128)S(1)} %psum.39, bf16[1024,128]{1,0:T(8,128)(2,1)S(1)} %copy-done.3, f32[2,768,128]{2,1,0:T(8,128)} %get-tuple-element.38, ...), kind=kOutput, calls=%fused_computation.2 | convolution fusion | flops 407963264 | bytes 12854272 | tf_op jit(solution)/shard_map/dot_general | solution.py:147
  240.0 6.2 %convolution_convert_fusion = bf16[2,768,1024]{2,1,0:T(8,128)(2,1)} fusion(bf16[16,8,2,1024]{3,1,2,0:T(8,128)(2,1)} %all-to-all-done.3, f32[2,768]{1,0:T(2,128)S(1)} %copy-done.10, f32[2,768,128]{2,1,0:T(8,128)} %copy-done.1), kind=kOutput, calls=%fused_computation.3 | convolution fusion | flops 404817536 | bytes 4462592 | tf_op jit(solution)/shard_map/cts,scd->ctd/dot_general | solution.py:134
  246.2 117.1 %all-reduce.3.cloned.1.call-done = f32[1024,128]{0,1:T(8,128)} async-done(((f32[1024,128]{0,1:T(8,128)}), f32[1024,128]{0,1:T(8,128)}) %all-reduce.3.cloned.1.call-update) | async-done | bytes 524304
  (70 shorter events, 41.2 us)
Async XLA Ops:
  7.2 1.9 copy-start
  11.0 39.5 %copy-start.1 = (f32[2,768,128]{2,1,0:T(8,128)}, f32[2,768,128]{2,1,0:T(8,128)S(1)}, u32[]{:S(2)}) copy-start(f32[2,768,128]{2,1,0:T(8,128)S(1)} %get-tuple-element.40) | copy-start | bytes 2359300
  12.2 38.3 %copy-start.9 = (f32[2,768]{1,0:T(2,128)}, f32[2,768]{1,0:T(2,128)S(1)}, u32[]{:S(2)}) copy-start(f32[2,768]{1,0:T(2,128)S(1)} %get-tuple-element.37) | copy-start | bytes 18436
  48.3 0.6 copy-start.5
  48.3 2.2 copy-start.7
  114.7 4.4 %copy-start.2 = (bf16[2,1024,512]{2,1,0:T(8,128)(2,1)S(1)}, bf16[2,1024,512]{2,1,0:T(8,128)(2,1)}, u32[]{:S(2)}) copy-start(bf16[2,1024,512]{2,1,0:T(8,128)(2,1)} %param.7) | copy-start | bytes 6291460
  120.6 9.6 %all-to-all-start.4 = ((bf16[8,2,8,1024]{3,2,1,0:T(8,128)(2,1)}), bf16[8,2,8,1024]{3,2,1,0:T(8,128)(2,1)S(1)}, u32[]{:S(2)}, u32[]{:S(2)}) async-start(bf16[8,2,8,1024]{3,2,1,0:T(8,128)(2,1)} %broadcast_in_dim.25), calls=%async_computation.4 | async-start | bytes 524288 | tf_op jit(solution)/shard_map/all_to_all | solution.py:53
  130.2 0.8 copy-start.4
  130.9 9.5 %all-to-all-start.2 = ((bf16[8,2,8,1024]{3,2,1,0:T(8,128)(2,1)}), bf16[8,2,8,1024]{3,2,1,0:T(8,128)(2,1)S(1)}, u32[]{:S(2)}, u32[]{:S(2)}) async-start(bf16[8,2,8,1024]{3,2,1,0:T(8,128)(2,1)} %broadcast_in_dim.11), calls=%async_computation.2 | async-start | bytes 524288 | tf_op jit(solution)/shard_map/all_to_all | solution.py:53
  141.3 19.9 %all-to-all-start.5 = ((bf16[16,8,2,1024]{3,1,2,0:T(8,128)(2,1)}), bf16[16,8,2,1024]{3,1,2,0:T(8,128)(2,1)}, u32[]{:S(2)}, u32[]{:S(2)}) async-start(bf16[16,8,2,1024]{3,1,2,0:T(8,128)(2,1)} %broadcast_in_dim.26), calls=%async_computation.5 | async-start | bytes 1048576 | tf_op jit(solution)/shard_map/all_to_all | solution.py:53
  149.6 19.6 %copy-start.6 = (f32[2,128]{1,0:T(2,128)S(1)}, f32[2,128]{1,0:T(2,128)}, u32[]{:S(2)}) copy-start(f32[2,128]{1,0:T(2,128)} %copy-done.5) | copy-start | bytes 3076
  149.6 19.6 %copy-start.8 = (f32[2,128]{1,0:T(2,128)S(1)}, f32[2,128]{1,0:T(2,128)}, u32[]{:S(2)}) copy-start(f32[2,128]{1,0:T(2,128)} %copy-done.7) | copy-start | bytes 3076
  162.1 43.9 %all-to-all-start.3 = ((bf16[16,8,2,1024]{3,1,2,0:T(8,128)(2,1)}), bf16[16,8,2,1024]{3,1,2,0:T(8,128)(2,1)}, u32[]{:S(2)}, u32[]{:S(2)}) async-start(bf16[16,8,2,1024]{3,1,2,0:T(8,128)(2,1)} %broadcast_in_dim.24), calls=%async_computation.3 | async-start | bytes 1048576 | tf_op jit(solution)/shard_map/all_to_all | solution.py:53
  167.1 196.3 %all-reduce.3.cloned.1.call-start = ((), (), s32[]{:S(2)}) async-start(), calls=%async_computation.6 | async-start | bytes 1048576
  172.4 37.5 %copy-start.10 = (f32[2,768]{1,0:T(2,128)S(1)}, f32[2,768]{1,0:T(2,128)}, u32[]{:S(2)}) copy-start(f32[2,768]{1,0:T(2,128)} %copy-done.9) | copy-start | bytes 18436
  221.3 5.0 %copy-start.3 = (bf16[1024,128]{1,0:T(8,128)(2,1)S(1)}, bf16[1024,128]{1,0:T(8,128)(2,1)}, u32[]{:S(2)}) copy-start(bf16[1024,128]{1,0:T(8,128)(2,1)} %param.6) | copy-start | bytes 786436
Sparse Core Ops, SparseCore 0:
  221.5 141.8 all-reduce.2
where the time goes:
time: 373 us; the launch traced here: 372 us
  waiting for transfers between devices  134 us (36%)
  blocking collectives  122 us (33%)
  matrix products  64.6 us (17%)
  starting transfers between devices  20.2 us (5%)
  between operations  14.2 us (4%)
  local copies, waits for them, and re-layouts  9.2 us (2%)
  other arithmetic  7.13 us (2%)
    unnamed x2, waiting for transfers between devices  117 us
    all_gather x5, blocking collectives, gathered_once(): both, at, found = (lax.all_gather(jnp.concatenate(lines), axis), 0, {})  35.8 us
    all_to_all x1, blocking collectives, sent_and_summed(): lax.all_to_all(parts, axis, split_axis=0, concat_axis=0, tiled=True)  34.8 us
    psum x5, blocking collectives, by_axis(): return functools.reduce(lax.psum, axes, array)  33.5 us
    all_to_all x4, starting transfers between devices, from_everyone(): return lax.all_to_all(copies, axis, split_axis=0, concat_axis=0, tiled=True)  20.2 us
    all_to_all x1, blocking collectives, from_everyone(): return lax.all_to_all(copies, axis, split_axis=0, concat_axis=0, tiled=True)  17.9 us
    all_to_all x4, waiting for transfers between devices, from_everyone(): return lax.all_to_all(copies, axis, split_axis=0, concat_axis=0, tiled=True)  17.3 us
    dot_general x1, matrix products, on_device(): jnp.dot(logit_b.reshape(clips * tok_rows, slot_total), router.T, preferre...  13.7 us
  transfers between devices with their start and end apart: 5, of which 4 were waited for; matrix products, arithmetic and copies ran while one was open for 10% of the time, Pallas kernels for 0%

commit v1 on v0

v1 whole, which is shorter than its diff:
```python
import functools

import jax
import jax.numpy as jnp
from jax import lax
from jax.experimental import pallas as pl
from jax.experimental.pallas import tpu as pltpu
from jax.sharding import Mesh
from jax.sharding import PartitionSpec as P

SEQ = ("seq_0", "seq_1")
EXP = ("exp_0", "exp_1", "exp_2")
CHIPS_EXP = ("exp_0", "exp_1")
CORE = "exp_2"
SEQ_EXP = SEQ + EXP

F32 = jnp.float32
BF16 = jnp.bfloat16
LANES = 128
GROUP = 8


def dot_nt(a, b):
    return lax.dot_general(a, b, (((1,), (1,)), ((), ())), preferred_element_type=F32)


def dot_nn(a, b):
    return lax.dot_general(a, b, (((1,), (0,)), ((), ())), preferred_element_type=F32)


def dot_tn(a, b):
    return lax.dot_general(a, b, (((0,), (0,)), ((), ())), preferred_element_type=F32)


def params(mib, grid_dims=0):
    kinds = ("arbitrary",) * grid_dims if grid_dims else None
    return pltpu.CompilerParams(vmem_limit_bytes=mib << 20, dimension_semantics=kinds)


def pieces(value, count):
    found = []
    for _ in range(count):
        part = value.astype(BF16).astype(F32)
        found.append(part)
        value = value - part
    return found


def packed(columns):
    rows = columns[0].shape[0]
    lane = lax.broadcasted_iota(jnp.int32, (rows, LANES), 1)
    tile = jnp.zeros((rows, LANES), F32)
    for k, column in enumerate(columns):
        tile = jnp.where(lane == k, column, tile)
    return tile


def mixing_of(logits_t):
    peak = jnp.max(logits_t, axis=0, keepdims=True)
    terms = jnp.exp(logits_t - peak)
    return terms / jnp.sum(terms, axis=0, keepdims=True)


def first_pass(tok_ref, router_ref, grad_ref, logits_ref, router_t_ref, send_ref, keep_ref, sums, stats):
    clip = pl.program_id(0)
    core = lax.axis_index(CORE)
    width = tok_ref.shape[2]

    @pl.when(clip == 0)
    def _():
        router_t_ref[...] = router_ref[...].T

    tok = tok_ref[0]
    logits_t = dot_nt(router_t_ref[...], tok)
    logits_ref[0] = logits_t
    peak = jnp.max(logits_t, axis=1, keepdims=True).astype(BF16).astype(F32)
    terms = jnp.exp(logits_t - peak)
    mass = jnp.sum(terms, axis=1, keepdims=True)
    sums[0] = dot_nn(terms.astype(BF16), tok)
    sums[1] = dot_nn(mixing_of(logits_t).astype(BF16), grad_ref[0])
    columns = [peak] + pieces(mass, 2)
    lane = lax.broadcasted_iota(jnp.int32, stats.shape, 1)
    for c in range(2):

        @pl.when(clip == c)
        def _(c=c):
            old = jnp.zeros(stats.shape, F32) if c == 0 else stats[...]
            for k, column in zip((c, 2 + 2 * c, 3 + 2 * c), columns):
                old = jnp.where(lane == k, column, old)
            stats[...] = old
            for q in range(send_ref.shape[0]):
                mine = pl.ds(pl.multiple_of((2 * q + core) * GROUP, GROUP), GROUP)
                other = pl.ds(pl.multiple_of((2 * q + 1 - core) * GROUP, GROUP), GROUP)
                for part in range(2):
                    at = pl.ds((2 * part + c) * width, width)
                    keep_ref[q, :, at] = sums[part, mine, :].astype(BF16)
                    send_ref[q, :, at] = sums[part, other, :].astype(BF16)
                if c == 1:
                    keep_ref[q, :, pl.ds(4 * width, LANES)] = stats[mine, :].astype(BF16)
                    send_ref[q, :, pl.ds(4 * width, LANES)] = stats[other, :].astype(BF16)


def run_first_pass(tokens, router, grad_out):
    clips, rows, width = tokens.shape
    slots = router.shape[1]
    row = 4 * width + LANES
    groups = slots // GROUP // 2
    whole = lambda *shape: pl.BlockSpec(shape, lambda c: (0,) * len(shape))
    per_clip = lambda *shape: pl.BlockSpec((1, *shape), lambda c: (c, 0, 0))
    return pl.pallas_call(
        first_pass,
        grid=(clips,),
        in_specs=[per_clip(rows, width), whole(width, slots), per_clip(rows, width)],
        out_specs=[
            per_clip(slots, rows),
            whole(slots, width),
            whole(groups, GROUP, row),
            whole(groups, GROUP, row),
        ],
        out_shape=[
            jax.ShapeDtypeStruct((clips, slots, rows), F32),
            jax.ShapeDtypeStruct((slots, width), BF16),
            jax.ShapeDtypeStruct((groups, GROUP, row), BF16),
            jax.ShapeDtypeStruct((groups, GROUP, row), BF16),
        ],
        scratch_shapes=[pltpu.VMEM((2, slots, width), F32), pltpu.VMEM((slots, LANES), F32)],
        compiler_params=params(28, 1),
        name="first_pass",
    )(tokens, router, grad_out)


def merged(blocks, width):
    tiles = [load(4 * width, LANES) for load in blocks]
    top = functools.reduce(jnp.maximum, tiles)
    scales = [jnp.exp(jnp.minimum(tile - top, 0.0)) for tile in tiles]
    inputs, grads, peaks, masses = [], [], [], []
    for c in range(2):
        peaks.append(top[:, c : c + 1])
        columns = [scale[:, c : c + 1] for scale in scales]
        masses.append(
            sum(col * (t[:, 2 + 2 * c : 3 + 2 * c] + t[:, 3 + 2 * c : 4 + 2 * c]) for col, t in zip(columns, tiles))
        )
        inputs.append(sum(col * load(c * width, width) for col, load in zip(columns, blocks)))
        grads.append(sum(load((2 + c) * width, width) for load in blocks))
    return inputs, grads, peaks, masses


def loader(ref, index):
    return lambda at, size: ref[index, :, pl.ds(at, size)].astype(F32)


def stat_tile(peaks, masses):
    return packed([peaks[0], peaks[1], *pieces(masses[0], 2), *pieces(masses[1], 2)])


def merge_cores(keep_ref, recv_ref, out_ref):
    width = (keep_ref.shape[2] - LANES) // 4
    for q in range(keep_ref.shape[0]):
        inputs, grads, peaks, masses = merged([loader(keep_ref, q), loader(recv_ref, q)], width)
        for k, value in enumerate(inputs + grads):
            out_ref[q, :, pl.ds(k * width, width)] = value.astype(BF16)
        out_ref[q, :, pl.ds(4 * width, LANES)] = stat_tile(peaks, masses).astype(BF16)


def merge_column(in_ref, out_ref):
    width = (in_ref.shape[2] - LANES) // 4
    blocks = [loader(in_ref, k) for k in range(in_ref.shape[0])]
    inputs, grads, peaks, masses = merged(blocks, width)
    for k, value in enumerate(inputs + grads):
        for q in range(out_ref.shape[0]):
            out_ref[q, :, pl.ds(k * width, width)] = value.astype(BF16)
    for q in range(out_ref.shape[0]):
        out_ref[q, :, pl.ds(4 * width, LANES)] = stat_tile(peaks, masses).astype(BF16)


GELU_A = 0.7978845608028654
GELU_B = 0.044715


def experts(in_ref, w_in_ref, w_out_ref, out_ref, rows_ref, grads_ref, hidden_ref, pre_grad_ref, slot_in_ref, stats_ref):
    width = w_in_ref.shape[1]
    count = w_in_ref.shape[0]
    blocks = [loader(in_ref, k) for k in range(in_ref.shape[0])]
    inputs, grads, peaks, masses = merged(blocks, width)
    slot_in = jnp.concatenate([value / mass for value, mass in zip(inputs, masses)], axis=0)
    slot_in_ref[...] = slot_in
    stats_ref[...] = packed([*peaks, *pieces(masses[0], 3), *pieces(masses[1], 3)])
    x = slot_in.astype(BF16)
    g = jnp.concatenate(grads, axis=0).astype(BF16)
    rows_ref[...] = x
    grads_ref[...] = g
    total = x.shape[0]
    hid = w_in_ref.shape[2]
    owner = lambda shape: lax.rem(lax.broadcasted_iota(jnp.int32, shape, 0), GROUP) // (GROUP // count)
    who = owner((total, hid))
    pre = jnp.zeros((total, hid), F32)
    hidden_grad = jnp.zeros((total, hid), F32)
    for e in range(count):
        pre = jnp.where(who == e, dot_nn(x, w_in_ref[e]), pre)
        hidden_grad = jnp.where(who == e, dot_nt(g, w_out_ref[e]), hidden_grad)
    inner = jnp.tanh(GELU_A * (pre + GELU_B * pre * pre * pre))
    hidden = 0.5 * pre * (1.0 + inner)
    slope = 0.5 * (1.0 + inner) + 0.5 * pre * (1.0 - inner * inner) * GELU_A * (1.0 + 3.0 * GELU_B * pre * pre)
    pre_grad = hidden_grad * slope
    hidden_ref[...] = hidden.astype(BF16)
    pre_grad_ref[...] = pre_grad.astype(BF16)
    out_part = jnp.zeros((total, width), F32)
    in_part = jnp.zeros((total, width), F32)
    for e in range(count):
        out_part += dot_nn(jnp.where(who == e, hidden, 0.0).astype(BF16), w_out_ref[e])
        in_part += dot_nt(jnp.where(who == e, pre_grad, 0.0).astype(BF16), w_in_ref[e])
    both = jnp.concatenate([out_part, in_part], axis=0).astype(BF16)
    for q in range(out_ref.shape[0]):
        out_ref[q] = both


def run_experts(sums, w_in, w_out):
    count, width, hid = w_in.shape
    peers = sums.shape[0]
    rows = 2 * GROUP
    return pl.pallas_call(
        experts,
        out_shape=[
            jax.ShapeDtypeStruct((peers, 2 * rows, width), BF16),
            jax.ShapeDtypeStruct((rows, width), BF16),
            jax.ShapeDtypeStruct((rows, width), BF16),
            jax.ShapeDtypeStruct((rows, hid), BF16),
            jax.ShapeDtypeStruct((rows, hid), BF16),
            jax.ShapeDtypeStruct((rows, width), F32),
            jax.ShapeDtypeStruct((GROUP, LANES), F32),
        ],
        compiler_params=params(16),
        name="experts",
    )(sums, w_in, w_out)


def weight_grads(rows_ref, grads_ref, hidden_ref, pre_grad_ref, w_in_grad_ref, w_out_grad_ref):
    e = pl.program_id(0)
    total, hid = hidden_ref.shape
    count = pl.num_programs(0)
    who = lax.rem(lax.broadcasted_iota(jnp.int32, (total, hid), 0), GROUP) // (GROUP // 2)
    mask = who == e
    hidden = jnp.where(mask, hidden_ref[...].astype(F32), 0.0).astype(BF16)
    pre_grad = jnp.where(mask, pre_grad_ref[...].astype(F32), 0.0).astype(BF16)
    w_out_grad_ref[0] = dot_tn(hidden, grads_ref[...]).astype(BF16)
    w_in_grad_ref[0] = dot_tn(rows_ref[...], pre_grad).astype(BF16)


def run_weight_grads(rows, grads, hidden, pre_grad, count):
    total, width = rows.shape
    hid = hidden.shape[1]
    whole = lambda *shape: pl.BlockSpec(shape, lambda e: (0,) * len(shape))
    return pl.pallas_call(
        weight_grads,
        grid=(count,),
        in_specs=[whole(total, width), whole(total, width), whole(total, hid), whole(total, hid)],
        out_specs=[
            pl.BlockSpec((1, width, hid), lambda e: (e, 0, 0)),
            pl.BlockSpec((1, hid, width), lambda e: (e, 0, 0)),
        ],
        out_shape=[
            jax.ShapeDtypeStruct((count, width, hid), BF16),
            jax.ShapeDtypeStruct((count, hid, width), BF16),
        ],
        compiler_params=params(16, 1),
        cost_estimate=pl.CostEstimate(
            flops=4 * count * total * width * hid, transcendentals=0, bytes_accessed=4 * count * width * hid
        ),
        name="weight_grads",
    )(rows, grads, hidden, pre_grad)


def slot_results(in_ref, slot_in_ref, stats_ref, out_ref):
    width = in_ref.shape[2]
    total = sum(in_ref[k].astype(F32) for k in range(in_ref.shape[0])).astype(BF16)
    back = total[2 * GROUP :].astype(F32)
    inner = jnp.sum(back * slot_in_ref[...], axis=1, keepdims=True)
    tile = stats_ref[...]
    lane = lax.broadcasted_iota(jnp.int32, tile.shape, 1)
    for c in range(2):
        for k, column in enumerate(pieces(inner[c * GROUP : (c + 1) * GROUP], 3)):
            tile = jnp.where(lane == 8 + 3 * c + k, column, tile)
    for q in range(out_ref.shape[0]):
        for k in range(4):
            out_ref[q, :, pl.ds(k * width, width)] = total[k * GROUP : (k + 1) * GROUP]
        out_ref[q, :, pl.ds(4 * width, LANES)] = tile.astype(BF16)


def second_pass(
    tok_ref, grad_ref, logits_ref, router_t_ref, mine_ref, other_ref,
    outs_ref, backs_ref, mix_ref, weights_ref, part_ref, stats, total,
):
    clip = pl.program_id(0)
    core = lax.axis_index(CORE)
    width = tok_ref.shape[2]
    slots = logits_ref.shape[1]

    @pl.when(clip == 0)
    def _():
        for way in range(2):

            @pl.when(core == way)
            def _(way=way):
                pair = (mine_ref, other_ref) if way == 0 else (other_ref, mine_ref)
                for q in range(mine_ref.shape[0]):
                    for half in range(2):
                        at = pl.ds((2 * q + half) * GROUP, GROUP)
                        for c in range(2):
                            outs_ref[c, at, :] = pair[half][q, :, pl.ds(c * width, width)]
                            backs_ref[c, at, :] = pair[half][q, :, pl.ds((2 + c) * width, width)]
                        stats[at, :] = pair[half][q, :, pl.ds(4 * width, LANES)].astype(F32)

        for c in range(2):
            backs_ref[c, pl.ds(slots, slots), :] = router_t_ref[...]
        total[...] = jnp.zeros_like(total)

    tile = stats[...]
    column = lambda k: jnp.where(clip == 0, tile[:, k[0] : k[0] + 1], tile[:, k[1] : k[1] + 1])
    peak = column((0, 1))
    mass = column((2, 5)) + column((3, 6)) + column((4, 7))
    inner = column((8, 11)) + column((9, 12)) + column((10, 13))
    logits_t = logits_ref[0]
    dispatch = jnp.exp(logits_t - peak) / mass
    mixing = mixing_of(logits_t)
    mix_ref[0] = mixing.astype(BF16)
    tok = tok_ref[0]
    dispatch_grad = dot_nt(backs_ref[clip, pl.ds(0, slots), :], tok)
    mixing_grad = dot_nt(outs_ref[clip], grad_ref[0])
    logit_grad = dispatch * (dispatch_grad - inner) + mixing * (
        mixing_grad - jnp.sum(mixing * mixing_grad, axis=0, keepdims=True)
    )
    logit_b = logit_grad.astype(BF16)
    weights_ref[0, pl.ds(0, slots), :] = dispatch.astype(BF16)
    weights_ref[0, pl.ds(slots, slots), :] = logit_b
    total[...] += dot_nn(logit_b, tok)

    @pl.when(clip == pl.num_programs(0) - 1)
    def _():
        part_ref[...] = total[...].T.astype(BF16)


def run_second_pass(tokens, grad_out, logits, router_t, mine, other):
    clips, rows, width = tokens.shape
    slots = router_t.shape[0]
    whole = lambda *shape: pl.BlockSpec(shape, lambda c: (0,) * len(shape))
    per_clip = lambda *shape: pl.BlockSpec((1, *shape), lambda c: (c, 0, 0))
    return pl.pallas_call(
        second_pass,
        grid=(clips,),
        in_specs=[
            per_clip(rows, width),
            per_clip(rows, width),
            per_clip(slots, rows),
            whole(slots, width),
            whole(*mine.shape),
            whole(*other.shape),
        ],
        out_specs=[
            whole(clips, slots, width),
            whole(clips, 2 * slots, width),
            per_clip(slots, rows),
            per_clip(2 * slots, rows),
            whole(width, slots),
        ],
        out_shape=[
            jax.ShapeDtypeStruct((clips, slots, width), BF16),
            jax.ShapeDtypeStruct((clips, 2 * slots, width), BF16),
            jax.ShapeDtypeStruct((clips, slots, rows), BF16),
            jax.ShapeDtypeStruct((clips, 2 * slots, rows), BF16),
            jax.ShapeDtypeStruct((width, slots), BF16),
        ],
        scratch_shapes=[pltpu.VMEM((slots, LANES), F32), pltpu.VMEM((slots, width), F32)],
        compiler_params=params(28, 1),
        name="second_pass",
    )(tokens, grad_out, logits, router_t, mine, other)


def token_outputs(mix_ref, weights_ref, outs_ref, backs_ref, mixed_ref, grad_tokens_ref):
    mixed_ref[0] = dot_tn(mix_ref[0], outs_ref[0]).astype(BF16)
    grad_tokens_ref[0] = dot_tn(weights_ref[0], backs_ref[0]).astype(BF16)


def run_token_outputs(mix, weights, outs, backs):
    clips, slots, rows = mix.shape
    width = outs.shape[2]
    block = 256
    out = pl.BlockSpec((1, block, width), lambda c, t: (c, t, 0))
    return pl.pallas_call(
        token_outputs,
        grid=(clips, rows // block),
        in_specs=[
            pl.BlockSpec((1, slots, block), lambda c, t: (c, 0, t)),
            pl.BlockSpec((1, 2 * slots, block), lambda c, t: (c, 0, t)),
            pl.BlockSpec((1, slots, width), lambda c, t: (c, 0, 0)),
            pl.BlockSpec((1, 2 * slots, width), lambda c, t: (c, 0, 0)),
        ],
        out_specs=[out, out],
        out_shape=[jax.ShapeDtypeStruct((clips, rows, width), BF16)] * 2,
        compiler_params=params(16, 2),
        cost_estimate=pl.CostEstimate(
            flops=6 * clips * rows * slots * width, transcendentals=0, bytes_accessed=6 * clips * rows * width
        ),
        name="token_outputs",
    )(mix, weights, outs, backs)


def add_up(in_ref, out_ref):
    out_ref[...] = jnp.sum(in_ref[...].astype(F32), axis=0)


def exchanged(array, axes):
    return lax.all_to_all(array, axes, split_axis=0, concat_axis=0, tiled=True)


def swapped(array):
    return lax.ppermute(array, CORE, [(0, 1), (1, 0)])


def on_device(tokens, router, w_in, w_out, grad_out):
    peers = lax.axis_size(SEQ)
    width = tokens.shape[2]
    row = 4 * width + LANES
    chips = lax.axis_size(CHIPS_EXP)
    logits, router_t, send, keep = run_first_pass(tokens, router, grad_out)
    recv = swapped(send)
    small = params(16)
    halves = pl.pallas_call(
        merge_cores, out_shape=jax.ShapeDtypeStruct((chips, GROUP, row), BF16), compiler_params=small, name="merge_cores"
    )(keep, recv)
    column = pl.pallas_call(
        merge_column, out_shape=jax.ShapeDtypeStruct((peers, GROUP, row), BF16), compiler_params=small, name="merge_column"
    )(exchanged(halves, CHIPS_EXP))
    parts, rows, grads, hidden, pre_grad, slot_in, stats = run_experts(exchanged(column, SEQ), w_in, w_out)
    arrived = exchanged(parts, SEQ)
    grad_w_in, grad_w_out = run_weight_grads(rows, grads, hidden, pre_grad, w_in.shape[0])
    results = pl.pallas_call(
        slot_results, out_shape=jax.ShapeDtypeStruct((chips, GROUP, row), BF16), compiler_params=small, name="slot_results"
    )(arrived, slot_in, stats)
    mine = exchanged(results, CHIPS_EXP)
    other = swapped(mine)
    outs, backs, mix, weights, part = run_second_pass(tokens, grad_out, logits, router_t, mine, other)
    devices = lax.axis_size(SEQ_EXP)
    arrived = exchanged(part.reshape(devices, width // devices, part.shape[1]), SEQ_EXP)
    mixed, grad_tokens = run_token_outputs(mix, weights, outs, backs)
    grad_router = pl.pallas_call(
        add_up, out_shape=jax.ShapeDtypeStruct(arrived.shape[1:], F32), compiler_params=small, name="add_up"
    )(arrived)
    return (mixed, grad_tokens, grad_router, grad_w_in, grad_w_out)


def solution(mesh):
    finer = Mesh(mesh.devices.reshape(2, 4, 2, 4, 2), SEQ_EXP)
    return jax.shard_map(
        on_device,
        mesh=finer,
        in_specs=(
            P(None, SEQ_EXP, None),
            P(),
            P(EXP, None, SEQ),
            P(EXP, SEQ, None),
            P(None, SEQ_EXP, None),
        ),
        out_specs=(
            P(None, SEQ_EXP, None),
            P(None, SEQ_EXP, None),
            P(SEQ_EXP, None),
            P(EXP, None, SEQ),
            P(EXP, SEQ, None),
        ),
        check_vma=False,
    )
```

time: 373 us -> 95.2 us (0.26)
  waiting for transfers between devices: 134 us -> 7.2 us
  blocking collectives: 122 us -> 54.6 us
  matrix products: 64.6 us -> 0 us
  Pallas kernels: 0 us -> 17.7 us
  between operations: 14.2 us -> 0.71 us
  starting transfers between devices: 20.2 us -> 9.77 us
  other arithmetic: 7.13 us -> 0 us
  local copies, waits for them, and re-layouts: 9.2 us -> 4.74 us
    unnamed x2 -> x0, waiting for transfers between devices: 117 us -> none
    dot_general x15 -> x0, matrix products: 64.6 us -> none  [the longest x1 13.7 us: on_device(): jnp.dot(logit_b.reshape(clips * tok_rows, slot_total), router.T, preferre...]
    all_gather x5 -> x0, blocking collectives: 35.8 us -> none  [gathered_once(): both, at, found = (lax.all_gather(jnp.concatenate(lines), axis), 0, {})]
    psum x5 -> x0, blocking collectives: 33.5 us -> none  [by_axis(): return functools.reduce(lax.psum, axes, array)]
    pallas_call x0 -> x9, Pallas kernels: none -> 17.7 us  [the longest x1 4.42 us: run_token_outputs(): pl.pallas_call(token_outputs, grid=(clips, rows // block), in_specs=[pl.B...]
    all_to_all x4 -> x1, starting transfers between devices: 20.2 us -> 3.77 us  [exchanged(): return lax.all_to_all(array, axes, split_axis=0, concat_axis=0, tiled=True)]
    all_to_all x4 -> x1, waiting for transfers between devices: 17.3 us -> 4.08 us  [exchanged(): return lax.all_to_all(array, axes, split_axis=0, concat_axis=0, tiled=True)]
    ppermute x0 -> x2, starting transfers between devices: none -> 6 us  [swapped(): return lax.ppermute(array, CORE, [(0, 1), (1, 0)])]
  transfers between devices with their start and end apart: 5 -> 3, of which waited for: 4 -> 3; matrix products, arithmetic and copies ran while one was open for 10% -> 0% of each run, Pallas kernels for 0% -> 7%
where the time goes in v1:
time: 95.2 us; the launch traced here: 94.8 us
  blocking collectives  54.6 us (57%)
  Pallas kernels  17.7 us (19%)
  starting transfers between devices  9.77 us (10%)
  waiting for transfers between devices  7.2 us (8%)
  local copies, waits for them, and re-layouts  4.74 us (5%)
    all_to_all x4, blocking collectives, exchanged(): return lax.all_to_all(array, axes, split_axis=0, concat_axis=0, tiled=True)  54.6 us
    ppermute x2, starting transfers between devices, swapped(): return lax.ppermute(array, CORE, [(0, 1), (1, 0)])  6 us
    unnamed x12, local copies, waits for them, and re-layouts  4.74 us
    pallas_call x1, Pallas kernels, run_token_outputs(): pl.pallas_call(token_outputs, grid=(clips, rows // block), in_specs=[pl.B...  4.42 us
    all_to_all x1, waiting for transfers between devices, exchanged(): return lax.all_to_all(array, axes, split_axis=0, concat_axis=0, tiled=True)  4.08 us
    pallas_call x1, Pallas kernels, run_second_pass(): pl.pallas_call(second_pass, grid=(clips,), in_specs=[per_clip(rows, width...  4.01 us
    all_to_all x1, starting transfers between devices, exchanged(): return lax.all_to_all(array, axes, split_axis=0, concat_axis=0, tiled=True)  3.77 us
    pallas_call x1, Pallas kernels, run_first_pass(): pl.pallas_call(first_pass, grid=(clips,), in_specs=[per_clip(rows, width)...  3.35 us
  transfers between devices with their start and end apart: 3, of which 3 were waited for; matrix products, arithmetic and copies ran while one was open for 0% of the time, Pallas kernels for 7%

profile of v1, /device:TPU:1, one launch (start us, length us, event | category | flops | bytes accessed | tf_op | source)
XLA Modules:
  0.0 94.8 jit_solution(4035216578925346647)
XLA Ops:
  0.6 1.9 %copy-done = bf16[2,768,1024]{2,1,0:T(8,128)(2,1)S(1)} copy-done((bf16[2,768,1024]{2,1,0:T(8,128)(2,1)S(1)}, bf16[2,768,1024]{2,1,0:T(8,128)(2,1)}, u32[]{:S(2)}) %copy-start) | copy-done | bytes 3145752
  2.5 1.9 %copy-done.1 = bf16[2,768,1024]{2,1,0:T(8,128)(2,1)S(1)} copy-done((bf16[2,768,1024]{2,1,0:T(8,128)(2,1)S(1)}, bf16[2,768,1024]{2,1,0:T(8,128)(2,1)}, u32[]{:S(2)}) %copy-start.1) | copy-done | bytes 3145752
  4.4 0.9 %copy-done.5 = bf16[1024,128]{1,0:T(8,128)(2,1)S(1)} copy-done((bf16[1024,128]{1,0:T(8,128)(2,1)S(1)}, bf16[1024,128]{1,0:T(8,128)(2,1)}, u32[]{:S(2)}) %copy-start.5) | copy-done | bytes 262168
  5.4 3.4 %first_pass.1 = (f32[2,128,768]{2,1,0:T(8,128)S(1)}, bf16[128,1024]{1,0:T(8,128)(2,1)S(1)}, bf16[8,8,4224]{2,1,0:T(8,128)(2,1)S(1)}, bf16[8,8,4224]{2,1,0:T(8,128)(2,1)S(1)}) custom-call(bf16[2,768,1024]{2,1,0:T(8,128)(2,1)S(1)} %copy-done, bf16[1024,128]{1,0:T(8,128)(2,1)S(1)} %copy-done.5, bf16[2,768,1024]{2,1,0:T(8,128)(2,1)S(1)} %copy-done.1), custom_call_target="tpu_custom_call" | custom-call | tf_op jit(solution)/shard_map/first_pass/pallas_call | solution.py:110
  8.7 0.0 copy-start.3
  8.7 0.0 copy-start.4
  8.7 1.5 %collective-permute-start = (bf16[8,8,4224]{2,1,0:T(8,128)(2,1)S(1)}, bf16[8,8,4224]{2,1,0:T(8,128)(2,1)S(1)}, u32[]{:S(2)}, u32[]{:S(2)}) collective-permute-start(bf16[8,8,4224]{2,1,0:T(8,128)(2,1)S(1)} %get-tuple-element.28), channel_id=1, source_target_pairs={{0,1},{1,0},{2,3},{3,2},{4,5},{5,4},{6,7},{7,6},{8,9},{9,8},{10,11... | collective-permute-start | bytes 1622024 | tf_op jit(solution)/shard_map/ppermute | solution.py:416
  10.2 1.6 %collective-permute-done.recv_ref = bf16[8,8,4224]{2,1,0:T(8,128)(2,1)S(1)} collective-permute-done((bf16[8,8,4224]{2,1,0:T(8,128)(2,1)S(1)}, bf16[8,8,4224]{2,1,0:T(8,128)(2,1)S(1)}, u32[]{:S(2)}, u32[]{:S(2)}) %collective-permute-start) | collective-permute-done | bytes 540704 | tf_op jit(solution)/shard_map/ppermute | solution.py:416
  11.8 0.3 merge_cores.1
  12.1 19.2 %all_to_all.25.in_ref = bf16[8,8,4224]{2,1,0:T(8,128)(2,1)S(1)} all-to-all(bf16[8,8,4224]{2,1,0:T(8,128)(2,1)S(1)} %merge_cores.1), channel_id=1, replica_groups=mesh['seq_0'=2,'seq_1'=4,'exp_0'=2,'exp_1'=4,'exp_2'=2] {'exp_0','exp_1'}, dimensions={0} | all-to-all | bytes 1081344 | tf_op jit(solution)/shard_map/all_to_all | solution.py:412
  31.3 0.3 merge_column.1
  31.6 13.2 %all_to_all.26.in_ref = bf16[8,8,4224]{2,1,0:T(8,128)(2,1)S(1)} all-to-all(bf16[8,8,4224]{2,1,0:T(8,128)(2,1)S(1)} %merge_column.1), channel_id=1, replica_groups=mesh['seq_0'=2,'seq_1'=4,'exp_0'=2,'exp_1'=4,'exp_2'=2] {'seq_0','seq_1'}, dimensions={0} | all-to-all | bytes 1081344 | tf_op jit(solution)/shard_map/all_to_all | solution.py:412
  44.8 2.0 %experts.1 = (bf16[8,32,1024]{2,1,0:T(8,128)(2,1)S(1)}, bf16[16,1024]{1,0:T(8,128)(2,1)S(1)}, bf16[16,1024]{1,0:T(8,128)(2,1)S(1)}, bf16[16,512]{1,0:T(8,128)(2,...) custom-call(bf16[8,8,4224]{2,1,0:T(8,128)(2,1)S(1)} %all_to_all.26.in_ref, ...), custom_call_target="tpu_custom_call" | custom-call | tf_op jit(solution)/shard_map/experts/pallas_call | solution.py:221
  46.8 10.4 %all_to_all.27.in_ref = bf16[8,32,1024]{2,1,0:T(8,128)(2,1)S(1)} all-to-all(bf16[8,32,1024]{2,1,0:T(8,128)(2,1)S(1)} %get-tuple-element.29), channel_id=1, replica_groups=mesh['seq_0'=2,'seq_1'=4,'exp_0'=2,'exp_1'=4,'exp_2'=2] {'seq_0','seq_1'}, dimensions={0} | all-to-all | bytes 1048576 | tf_op jit(solution)/shard_map/all_to_all | solution.py:412
  57.2 0.1 slot_results.1
  57.3 11.8 %all_to_all.28.mine_ref = bf16[8,8,4224]{2,1,0:T(8,128)(2,1)S(1)} all-to-all(bf16[8,8,4224]{2,1,0:T(8,128)(2,1)S(1)} %slot_results.1), channel_id=1, replica_groups=mesh['seq_0'=2,'seq_1'=4,'exp_0'=2,'exp_1'=4,'exp_2'=2] {'exp_0','exp_1'}, dimensions={0} | all-to-all | bytes 1081344 | tf_op jit(solution)/shard_map/all_to_all | solution.py:412
  69.1 4.5 %collective-permute-start.1 = (bf16[8,8,4224]{2,1,0:T(8,128)(2,1)S(1)}, bf16[8,8,4224]{2,1,0:T(8,128)(2,1)S(1)}, u32[]{:S(2)}, u32[]{:S(2)}) collective-permute-start(bf16[8,8,4224]{2,1,0:T(8,128)(2,1)S(1)} %all_to_all.28.mine_ref), channel_id=1, source_target_pairs={{0,1},{1,0},{2,3},{3,2},{4,5},{5,4},{6,7},{7,6},{8,9},{9,8},{10,11... | collective-permute-start | bytes 1622024 | tf_op jit(solution)/shard_map/ppermute | solution.py:416
  73.6 1.6 %collective-permute-done.1.other_ref = bf16[8,8,4224]{2,1,0:T(8,128)(2,1)S(1)} collective-permute-done((bf16[8,8,4224]{2,1,0:T(8,128)(2,1)S(1)}, bf16[8,8,4224]{2,1,0:T(8,128)(2,1)S(1)}, u32[]{:S(2)}, u32[]{:S(2)}) %collective-permute-start.1) | collective-permute-done | bytes 540704 | tf_op jit(solution)/shard_map/ppermute | solution.py:416
  75.2 4.0 %second_pass.1 = (bf16[2,128,1024]{2,1,0:T(8,128)(2,1)S(1)}, bf16[2,256,1024]{2,1,0:T(8,128)(2,1)S(1)}, bf16[2,128,768]{2,1,0:T(8,128)(2,1)S(1)}, bf16[2,256,768]{2,1,0:T(8,128)(2,1)S(1)}, bf16[1024,128]{1,0:T(8,128)(2,1)}) custom-call(bf16[2,768,1024]{2,1,0:T(8,128)(2,1)S(1)} %copy-done, bf16[2,768,1024]{2,1,0:T(8,128)(2,1)S(1)} %copy-done.2, ...), custom_call_target="tpu_custom_call" | custom-call | tf_op jit(solution)/shard_map/second_pass/pallas_call | solution.py:347
  79.2 3.8 %all-to-all-start.4 = ((bf16[128,8,128]{2,1,0:T(8,128)(2,1)}), bf16[128,8,128]{2,1,0:T(8,128)(2,1)S(1)}, u32[]{:S(2)}, u32[]{:S(2)}) async-start(bf16[128,8,128]{2,1,0:T(8,128)(2,1)} %bitcast), calls=%async_computation.4 | async-start | bytes 524288 | tf_op jit(solution)/shard_map/all_to_all | solution.py:412
  83.0 2.6 %weight_grads.1 = (bf16[2,1024,512]{2,1,0:T(8,128)(2,1)}, bf16[2,512,1024]{2,1,0:T(8,128)(2,1)}) custom-call(bf16[16,1024]{1,0:T(8,128)(2,1)S(1)} %get-tuple-element.39.rows_ref, bf16[16,1024]{1,0:T(8,128)(2,1)S(1)} %get-tuple-element.40.grads_ref, bf16[16,512]{1,0:T(8,128)(2,1)S(1)} %get-tuple-element.41.hidden_ref, ...), custom_call_target="tpu_custom_call" | custom-call | flops 67108864 | bytes 4194304 | tf_op jit(solution)/shard_map/weight_grads/pallas_call | solution.py:253
  85.5 4.4 %token_outputs.1 = (bf16[2,768,1024]{2,1,0:T(8,128)(2,1)}, bf16[2,768,1024]{2,1,0:T(8,128)(2,1)}) custom-call(bf16[2,128,768]{2,1,0:T(8,128)(2,1)S(1)} %get-tuple-element.32.mix_ref, bf16[2,256,768]{2,1,0:T(8,128)(2,1)S(1)} %get-tuple-element.33.weights_ref, bf16[2,128,1024]{2,1,0:T(8,128)(2,1)S(1)} %get-tuple-element.34.outs_ref, ...), custom_call_target="tpu_custom_call" | custom-call | flops 1207959552 | bytes 9437184 | tf_op jit(solution)/shard_map/token_outputs/pallas_call | solution.py:388
  90.0 4.1 %all-to-all-done.4.in_ref = bf16[128,8,128]{2,1,0:T(8,128)(2,1)S(1)} async-done(((bf16[128,8,128]{2,1,0:T(8,128)(2,1)}), bf16[128,8,128]{2,1,0:T(8,128)(2,1)S(1)}, u32[]{:S(2)}, u32[]{:S(2)}) %all-to-all-start.4) | async-done | bytes 262176 | tf_op jit(solution)/shard_map/all_to_all | solution.py:412
  94.0 0.7 add_up.1
  (7 shorter events, 0.0 us)
Async XLA Ops:
  0.6 1.9 %copy-start = (bf16[2,768,1024]{2,1,0:T(8,128)(2,1)S(1)}, bf16[2,768,1024]{2,1,0:T(8,128)(2,1)}, u32[]{:S(2)}) copy-start(bf16[2,768,1024]{2,1,0:T(8,128)(2,1)} %tok_ref.3) | copy-start | bytes 9437188
  2.5 1.9 %copy-start.1 = (bf16[2,768,1024]{2,1,0:T(8,128)(2,1)S(1)}, bf16[2,768,1024]{2,1,0:T(8,128)(2,1)}, u32[]{:S(2)}) copy-start(bf16[2,768,1024]{2,1,0:T(8,128)(2,1)} %grad_ref.3) | copy-start | bytes 9437188
  4.4 0.9 %copy-start.5 = (bf16[1024,128]{1,0:T(8,128)(2,1)S(1)}, bf16[1024,128]{1,0:T(8,128)(2,1)}, u32[]{:S(2)}) copy-start(bf16[1024,128]{1,0:T(8,128)(2,1)} %router_ref.1) | copy-start | bytes 786436
  8.7 36.1 %copy-start.3 = (bf16[2,1024,512]{2,1,0:T(8,128)(2,1)S(1)}, bf16[2,1024,512]{2,1,0:T(8,128)(2,1)}, u32[]{:S(2)}) copy-start(bf16[2,1024,512]{2,1,0:T(8,128)(2,1)} %w_in_ref.1) | copy-start | bytes 6291460
  8.7 36.1 %copy-start.4 = (bf16[2,512,1024]{2,1,0:T(8,128)(2,1)S(1)}, bf16[2,512,1024]{2,1,0:T(8,128)(2,1)}, u32[]{:S(2)}) copy-start(bf16[2,512,1024]{2,1,0:T(8,128)(2,1)} %w_out_ref.1) | copy-start | bytes 6291460
  8.7 3.1 %collective-permute-start = (bf16[8,8,4224]{2,1,0:T(8,128)(2,1)S(1)}, bf16[8,8,4224]{2,1,0:T(8,128)(2,1)S(1)}, u32[]{:S(2)}, u32[]{:S(2)}) collective-permute-start(bf16[8,8,4224]{2,1,0:T(8,128)(2,1)S(1)} %get-tuple-element.28), channel_id=1, source_target_pairs={{0,1},{1,0},{2,3},{3,2},{4,5},{5,4},{6,7},{7,6},{8,9},{9,8},{10,11... | collective-permute-start | bytes 1622024 | tf_op jit(solution)/shard_map/ppermute | solution.py:416
  44.8 30.4 %copy-start.2 = (bf16[2,768,1024]{2,1,0:T(8,128)(2,1)S(1)}, bf16[2,768,1024]{2,1,0:T(8,128)(2,1)}, u32[]{:S(2)}) copy-start(bf16[2,768,1024]{2,1,0:T(8,128)(2,1)} %grad_ref.3) | copy-start | bytes 9437188
  69.1 6.1 %collective-permute-start.1 = (bf16[8,8,4224]{2,1,0:T(8,128)(2,1)S(1)}, bf16[8,8,4224]{2,1,0:T(8,128)(2,1)S(1)}, u32[]{:S(2)}, u32[]{:S(2)}) collective-permute-start(bf16[8,8,4224]{2,1,0:T(8,128)(2,1)S(1)} %all_to_all.28.mine_ref), channel_id=1, source_target_pairs={{0,1},{1,0},{2,3},{3,2},{4,5},{5,4},{6,7},{7,6},{8,9},{9,8},{10,11... | collective-permute-start | bytes 1622024 | tf_op jit(solution)/shard_map/ppermute | solution.py:416
  79.2 14.8 %all-to-all-start.4 = ((bf16[128,8,128]{2,1,0:T(8,128)(2,1)}), bf16[128,8,128]{2,1,0:T(8,128)(2,1)S(1)}, u32[]{:S(2)}, u32[]{:S(2)}) async-start(bf16[128,8,128]{2,1,0:T(8,128)(2,1)} %bitcast), calls=%async_computation.4 | async-start | bytes 524288 | tf_op jit(solution)/shard_map/all_to_all | solution.py:412

commit v2 on v1

--- a/solution.py
+++ b/solution.py
@@ -61,43 +61,65 @@
     return terms / jnp.sum(terms, axis=0, keepdims=True)
 
 
-def first_pass(tok_ref, router_ref, grad_ref, logits_ref, router_t_ref, send_ref, keep_ref, sums, stats):
-    clip = pl.program_id(0)
+def first_pass(
+    tok_hbm, router_hbm, grad_hbm,
+    tok_ref, grad_ref, router_t_ref, terms_ref, mixing_ref, mix_ref, stats_ref, keep_ref, send_ref,
+    router_buf, router_f, sems,
+):
     core = lax.axis_index(CORE)
-    width = tok_ref.shape[2]
-
-    @pl.when(clip == 0)
-    def _():
-        router_t_ref[...] = router_ref[...].T
-
-    tok = tok_ref[0]
-    logits_t = dot_nt(router_t_ref[...], tok)
-    logits_ref[0] = logits_t
-    peak = jnp.max(logits_t, axis=1, keepdims=True).astype(BF16).astype(F32)
-    terms = jnp.exp(logits_t - peak)
-    mass = jnp.sum(terms, axis=1, keepdims=True)
-    sums[0] = dot_nn(terms.astype(BF16), tok)
-    sums[1] = dot_nn(mixing_of(logits_t).astype(BF16), grad_ref[0])
-    columns = [peak] + pieces(mass, 2)
-    lane = lax.broadcasted_iota(jnp.int32, stats.shape, 1)
-    for c in range(2):
-
-        @pl.when(clip == c)
-        def _(c=c):
-            old = jnp.zeros(stats.shape, F32) if c == 0 else stats[...]
-            for k, column in zip((c, 2 + 2 * c, 3 + 2 * c), columns):
-                old = jnp.where(lane == k, column, old)
-            stats[...] = old
-            for q in range(send_ref.shape[0]):
-                mine = pl.ds(pl.multiple_of((2 * q + core) * GROUP, GROUP), GROUP)
-                other = pl.ds(pl.multiple_of((2 * q + 1 - core) * GROUP, GROUP), GROUP)
-                for part in range(2):
-                    at = pl.ds((2 * part + c) * width, width)
-                    keep_ref[q, :, at] = sums[part, mine, :].astype(BF16)
-                    send_ref[q, :, at] = sums[part, other, :].astype(BF16)
-                if c == 1:
-                    keep_ref[q, :, pl.ds(4 * width, LANES)] = stats[mine, :].astype(BF16)
-                    send_ref[q, :, pl.ds(4 * width, LANES)] = stats[other, :].astype(BF16)
+    clips, rows, width = tok_ref.shape
+    slots = router_t_ref.shape[0]
+    half = slots // 2
+    copies = [pltpu.make_async_copy(router_hbm, router_buf, sems.at[0])]
+    for c in range(clips):
+        copies.append(pltpu.make_async_copy(tok_hbm.at[c], tok_ref.at[c], sems.at[1 + c]))
+    for c in range(clips):
+        copies.append(pltpu.make_async_copy(grad_hbm.at[c], grad_ref.at[c], sems.at[1 + clips + c]))
+    for copy in copies:
+        copy.start()
+    copies[0].wait()
+    router_f[...] = router_buf[...].T.astype(F32)
+    for k in range(slots // GROUP):
+        place = k % (half // GROUP)
+        side = core if k < half // GROUP else 1 - core
+        at = pl.ds(pl.multiple_of((2 * place + side) * GROUP, GROUP), GROUP)
+        router_t_ref[pl.ds(k * GROUP, GROUP), :] = router_f[at, :].astype(BF16)
+    columns = [None] * 6
+    for c in range(clips):
+        copies[1 + c].wait()
+        logits_t = dot_nt(router_t_ref[...], tok_ref[c])
+        peak = jnp.max(logits_t, axis=1, keepdims=True).astype(BF16).astype(F32)
+        terms = jnp.exp(logits_t - peak)
+        terms_ref[c] = terms
+        mass = jnp.sum(terms, axis=1, keepdims=True)
+        columns[c] = peak
+        columns[2 + 2 * c : 4 + 2 * c] = pieces(mass, 2)
+        sums = dot_nn(terms.astype(BF16), tok_ref[c]).astype(BF16)
+        mixing = mixing_of(logits_t)
+        mixing_ref[c] = mixing
+        mix_ref[c] = mixing.astype(BF16)
+        for q in range(keep_ref.shape[0]):
+            at = pl.ds(c * width, width)
+            keep_ref[q, :, at] = sums[q * GROUP : (q + 1) * GROUP]
+            send_ref[q, :, at] = sums[half + q * GROUP : half + (q + 1) * GROUP]
+    stats = packed(columns)
+    stats_ref[...] = stats
+    stats = stats.astype(BF16)
+    for q in range(keep_ref.shape[0]):
+        at = pl.ds(4 * width, LANES)
+        keep_ref[q, :, at] = stats[q * GROUP : (q + 1) * GROUP]
+        send_ref[q, :, at] = stats[half + q * GROUP : half + (q + 1) * GROUP]
+    for c in range(clips):
+        copies[1 + clips + c].wait()
+        sums = dot_nn(mix_ref[c], grad_ref[c]).astype(BF16)
+        for q in range(keep_ref.shape[0]):
+            at = pl.ds((2 + c) * width, width)
+            keep_ref[q, :, at] = sums[q * GROUP : (q + 1) * GROUP]
+            send_ref[q, :, at] = sums[half + q * GROUP : half + (q + 1) * GROUP]
+
+
+VMEM = pl.BlockSpec(memory_space=pltpu.VMEM)
+HBM = pl.BlockSpec(memory_space=pltpu.HBM)
 
 
 def run_first_pass(tokens, router, grad_out):
@@ -105,28 +127,30 @@
     slots = router.shape[1]
     row = 4 * width + LANES
     groups = slots // GROUP // 2
-    whole = lambda *shape: pl.BlockSpec(shape, lambda c: (0,) * len(shape))
-    per_clip = lambda *shape: pl.BlockSpec((1, *shape), lambda c: (c, 0, 0))
+    shapes = [
+        (tokens.shape, BF16),
+        (grad_out.shape, BF16),
+        ((slots, width), BF16),
+        ((clips, slots, rows), F32),
+        ((clips, slots, rows), F32),
+        ((clips, slots, rows), BF16),
+        ((slots, LANES), F32),
+        ((groups, GROUP, row), BF16),
+        ((groups, GROUP, row), BF16),
+    ]
     return pl.pallas_call(
         first_pass,
-        grid=(clips,),
-        in_specs=[per_clip(rows, width), whole(width, slots), per_clip(rows, width)],
-        out_specs=[
-            per_clip(slots, rows),
-            whole(slots, width),
-            whole(groups, GROUP, row),
-            whole(groups, GROUP, row),
+        in_specs=[HBM] * 3,
+        out_specs=[VMEM] * len(shapes),
+        out_shape=[jax.ShapeDtypeStruct(*shape) for shape in shapes],
+        scratch_shapes=[
+            pltpu.VMEM(router.shape, BF16),
+            pltpu.VMEM((slots, width), F32),
+            pltpu.SemaphoreType.DMA((1 + 2 * clips,)),
         ],
-        out_shape=[
-            jax.ShapeDtypeStruct((clips, slots, rows), F32),
-            jax.ShapeDtypeStruct((slots, width), BF16),
-            jax.ShapeDtypeStruct((groups, GROUP, row), BF16),
-            jax.ShapeDtypeStruct((groups, GROUP, row), BF16),
-        ],
-        scratch_shapes=[pltpu.VMEM((2, slots, width), F32), pltpu.VMEM((slots, LANES), F32)],
-        compiler_params=params(28, 1),
+        compiler_params=params(28),
         name="first_pass",
-    )(tokens, router, grad_out)
+    )(*(pltpu.with_memory_space_constraint(a, pltpu.HBM) for a in (tokens, router, grad_out)))
 
 
 def merged(blocks, width):
@@ -287,92 +311,62 @@
 
 
 def second_pass(
-    tok_ref, grad_ref, logits_ref, router_t_ref, mine_ref, other_ref,
-    outs_ref, backs_ref, mix_ref, weights_ref, part_ref, stats, total,
+    tok_ref, grad_ref, terms_ref, mixing_ref, local_ref, router_t_ref, mine_ref, other_ref,
+    outs_ref, backs_ref, weights_ref, part_ref, ordered,
 ):
-    clip = pl.program_id(0)
     core = lax.axis_index(CORE)
-    width = tok_ref.shape[2]
-    slots = logits_ref.shape[1]
-
-    @pl.when(clip == 0)
-    def _():
-        for way in range(2):
-
-            @pl.when(core == way)
-            def _(way=way):
-                pair = (mine_ref, other_ref) if way == 0 else (other_ref, mine_ref)
-                for q in range(mine_ref.shape[0]):
-                    for half in range(2):
-                        at = pl.ds((2 * q + half) * GROUP, GROUP)
-                        for c in range(2):
-                            outs_ref[c, at, :] = pair[half][q, :, pl.ds(c * width, width)]
-                            backs_ref[c, at, :] = pair[half][q, :, pl.ds((2 + c) * width, width)]
-                        stats[at, :] = pair[half][q, :, pl.ds(4 * width, LANES)].astype(F32)
-
-        for c in range(2):
-            backs_ref[c, pl.ds(slots, slots), :] = router_t_ref[...]
-        total[...] = jnp.zeros_like(total)
-
-    tile = stats[...]
-    column = lambda k: jnp.where(clip == 0, tile[:, k[0] : k[0] + 1], tile[:, k[1] : k[1] + 1])
-    peak = column((0, 1))
-    mass = column((2, 5)) + column((3, 6)) + column((4, 7))
-    inner = column((8, 11)) + column((9, 12)) + column((10, 13))
-    logits_t = logits_ref[0]
-    dispatch = jnp.exp(logits_t - peak) / mass
-    mixing = mixing_of(logits_t)
-    mix_ref[0] = mixing.astype(BF16)
-    tok = tok_ref[0]
-    dispatch_grad = dot_nt(backs_ref[clip, pl.ds(0, slots), :], tok)
-    mixing_grad = dot_nt(outs_ref[clip], grad_ref[0])
-    logit_grad = dispatch * (dispatch_grad - inner) + mixing * (
-        mixing_grad - jnp.sum(mixing * mixing_grad, axis=0, keepdims=True)
-    )
-    logit_b = logit_grad.astype(BF16)
-    weights_ref[0, pl.ds(0, slots), :] = dispatch.astype(BF16)
-    weights_ref[0, pl.ds(slots, slots), :] = logit_b
-    total[...] += dot_nn(logit_b, tok)
-
-    @pl.when(clip == pl.num_programs(0) - 1)
-    def _():
-        part_ref[...] = total[...].T.astype(BF16)
-
-
-def run_second_pass(tokens, grad_out, logits, router_t, mine, other):
-    clips, rows, width = tokens.shape
+    clips, rows, width = tok_ref.shape
+    slots = router_t_ref.shape[0]
+    half = slots // 2
+    tiles = []
+    for k, ref in enumerate((mine_ref, other_ref)):
+        for q in range(ref.shape[0]):
+            at = pl.ds(k * half + q * GROUP, GROUP)
+            for c in range(clips):
+                outs_ref[c, at, :] = ref[q, :, pl.ds(c * width, width)]
+                backs_ref[c, at, :] = ref[q, :, pl.ds((2 + c) * width, width)]
+            tiles.append(ref[q, :, pl.ds(4 * width, LANES)].astype(F32))
+    tile = jnp.concatenate(tiles, axis=0)
+    local = local_ref[...]
+    column = lambda k: tile[:, k : k + 1]
+    total = jnp.zeros((slots, width), F32)
+    for c in range(clips):
+        backs_ref[c, pl.ds(slots, slots), :] = router_t_ref[...]
+        mass = column(2 + 3 * c) + column(3 + 3 * c) + column(4 + 3 * c)
+        inner = column(8 + 3 * c) + column(9 + 3 * c) + column(10 + 3 * c)
+        scale = jnp.exp(local[:, c : c + 1] - column(c)) / mass
+        dispatch = terms_ref[c] * scale
+        weights_ref[c, pl.ds(0, slots), :] = dispatch.astype(BF16)
+        mixing = mixing_ref[c]
+        dispatch_grad = dot_nt(backs_ref[c, pl.ds(0, slots), :], tok_ref[c])
+        mixing_grad = dot_nt(outs_ref[c], grad_ref[c])
+        logit_grad = dispatch * (dispatch_grad - inner) + mixing * (
+            mixing_grad - jnp.sum(mixing * mixing_grad, axis=0, keepdims=True)
+        )
+        logit_b = logit_grad.astype(BF16)
+        weights_ref[c, pl.ds(slots, slots), :] = logit_b
+        total = total + dot_nn(logit_b, tok_ref[c])
+    for k in range(slots // GROUP):
+        place = k % (half // GROUP)
+        side = core if k < half // GROUP else 1 - core
+        at = pl.ds(pl.multiple_of((2 * place + side) * GROUP, GROUP), GROUP)
+        ordered[at, :] = total[k * GROUP : (k + 1) * GROUP]
+    part_ref[...] = ordered[...].T.astype(BF16)
+
+
+def run_second_pass(tok, grad, terms, mixing, local, router_t, mine, other):
+    clips, rows, width = tok.shape
     slots = router_t.shape[0]
-    whole = lambda *shape: pl.BlockSpec(shape, lambda c: (0,) * len(shape))
-    per_clip = lambda *shape: pl.BlockSpec((1, *shape), lambda c: (c, 0, 0))
+    shapes = [(clips, slots, width), (clips, 2 * slots, width), (clips, 2 * slots, rows), (width, slots)]
     return pl.pallas_call(
         second_pass,
-        grid=(clips,),
-        in_specs=[
-            per_clip(rows, width),
-            per_clip(rows, width),
-            per_clip(slots, rows),
-            whole(slots, width),
-            whole(*mine.shape),
-            whole(*other.shape),
-        ],
-        out_specs=[
-            whole(clips, slots, width),
-            whole(clips, 2 * slots, width),
-            per_clip(slots, rows),
-            per_clip(2 * slots, rows),
-            whole(width, slots),
-        ],
-        out_shape=[
-            jax.ShapeDtypeStruct((clips, slots, width), BF16),
-            jax.ShapeDtypeStruct((clips, 2 * slots, width), BF16),
-            jax.ShapeDtypeStruct((clips, slots, rows), BF16),
-            jax.ShapeDtypeStruct((clips, 2 * slots, rows), BF16),
-            jax.ShapeDtypeStruct((width, slots), BF16),
-        ],
-        scratch_shapes=[pltpu.VMEM((slots, LANES), F32), pltpu.VMEM((slots, width), F32)],
-        compiler_params=params(28, 1),
+        in_specs=[VMEM] * 8,
+        out_specs=[VMEM] * len(shapes),
+        out_shape=[jax.ShapeDtypeStruct(shape, BF16) for shape in shapes],
+        scratch_shapes=[pltpu.VMEM((slots, width), F32)],
+        compiler_params=params(28),
         name="second_pass",
-    )(tokens, grad_out, logits, router_t, mine, other)
+    )(tok, grad, terms, mixing, local, router_t, mine, other)
 
 
 def token_outputs(mix_ref, weights_ref, outs_ref, backs_ref, mixed_ref, grad_tokens_ref):
@@ -405,7 +399,11 @@
 
 
 def add_up(in_ref, out_ref):
-    out_ref[...] = jnp.sum(in_ref[...].astype(F32), axis=0)
+    rows, total = out_ref.shape[0], in_ref.shape[0]
+    row = lax.broadcasted_iota(jnp.int32, (rows, total), 0)
+    at = lax.broadcasted_iota(jnp.int32, (rows, total), 1)
+    pick = jnp.where(lax.rem(at, rows) == row, 1.0, 0.0).astype(BF16)
+    out_ref[...] = dot_nn(pick, in_ref[...])
 
 
 def exchanged(array, axes):
@@ -421,7 +419,7 @@
     width = tokens.shape[2]
     row = 4 * width + LANES
     chips = lax.axis_size(CHIPS_EXP)
-    logits, router_t, send, keep = run_first_pass(tokens, router, grad_out)
+    tok, grad, router_t, terms, mixing, mix, local, keep, send = run_first_pass(tokens, router, grad_out)
     recv = swapped(send)
     small = params(16)
     halves = pl.pallas_call(
@@ -438,13 +436,13 @@
     )(arrived, slot_in, stats)
     mine = exchanged(results, CHIPS_EXP)
     other = swapped(mine)
-    outs, backs, mix, weights, part = run_second_pass(tokens, grad_out, logits, router_t, mine, other)
+    outs, backs, weights, part = run_second_pass(tok, grad, terms, mixing, local, router_t, mine, other)
     devices = lax.axis_size(SEQ_EXP)
     arrived = exchanged(part.reshape(devices, width // devices, part.shape[1]), SEQ_EXP)
     mixed, grad_tokens = run_token_outputs(mix, weights, outs, backs)
     grad_router = pl.pallas_call(
         add_up, out_shape=jax.ShapeDtypeStruct(arrived.shape[1:], F32), compiler_params=small, name="add_up"
-    )(arrived)
+    )(arrived.reshape(width, part.shape[1]))
     return (mixed, grad_tokens, grad_router, grad_w_in, grad_w_out)
 
 

time: 95.2 us -> 91.5 us (0.961)
  local copies, waits for them, and re-layouts: 4.74 us -> 0.01 us
  Pallas kernels: 17.7 us -> 18.9 us
    unnamed x12 -> x4, local copies, waits for them, and re-layouts: 4.74 us -> 0.01 us
    pallas_call x2, Pallas kernels: 7.36 us -> 8.56 us  [the longest x1 4.93 us: run_first_pass(): pl.pallas_call(first_pass, in_specs=[HBM] * 3, out_specs=[VMEM] * len(sha...]
  transfers between devices with their start and end apart: 3 -> 3, of which waited for: 3 -> 3; matrix products, arithmetic and copies ran while one was open for 0% -> 0% of each run, Pallas kernels for 7% -> 8%
where the time goes in v2:
time: 91.5 us; the launch traced here: 91.2 us
  blocking collectives  54.6 us (60%)
  Pallas kernels  18.9 us (21%)
  starting transfers between devices  9.76 us (11%)
  waiting for transfers between devices  7.2 us (8%)
    all_to_all x4, blocking collectives, exchanged(): return lax.all_to_all(array, axes, split_axis=0, concat_axis=0, tiled=True)  54.6 us
    ppermute x2, starting transfers between devices, swapped(): return lax.ppermute(array, CORE, [(0, 1), (1, 0)])  5.99 us
    pallas_call x1, Pallas kernels, run_first_pass(): pl.pallas_call(first_pass, in_specs=[HBM] * 3, out_specs=[VMEM] * len(sha...  4.93 us
    pallas_call x1, Pallas kernels, run_token_outputs(): pl.pallas_call(token_outputs, grid=(clips, rows // block), in_specs=[pl.B...  4.42 us
    all_to_all x1, waiting for transfers between devices, exchanged(): return lax.all_to_all(array, axes, split_axis=0, concat_axis=0, tiled=True)  4.08 us
    all_to_all x1, starting transfers between devices, exchanged(): return lax.all_to_all(array, axes, split_axis=0, concat_axis=0, tiled=True)  3.77 us
    pallas_call x1, Pallas kernels, run_second_pass(): pl.pallas_call(second_pass, in_specs=[VMEM] * 8, out_specs=[VMEM] * len(s...  3.63 us
    ppermute x2, waiting for transfers between devices, swapped(): return lax.ppermute(array, CORE, [(0, 1), (1, 0)])  3.12 us
  transfers between devices with their start and end apart: 3, of which 3 were waited for; matrix products, arithmetic and copies ran while one was open for 0% of the time, Pallas kernels for 8%

profile of v2, /device:TPU:1, one launch (start us, length us, event | category | flops | bytes accessed | tf_op | source)
XLA Modules:
  0.0 91.2 jit_solution(5239026910739832209)
XLA Ops:
  0.6 4.9 %first_pass.1 = (bf16[2,768,1024]{2,1,0:T(8,128)(2,1)S(1)}, bf16[2,768,1024]{2,1,0:T(8,128)(2,1)S(1)}, bf16[128,1024]{1,0:T(8,128)(2,1)S(1)}, f32[2,128,768]{2,1...) custom-call(bf16[2,768,1024]{2,1,0:T(8,128)(2,1)} %tok_hbm.1, ...), custom_call_target="tpu_custom_call" | custom-call | tf_op jit(solution)/shard_map/first_pass/pallas_call | solution.py:141
  5.6 0.0 copy-start
  5.6 0.0 copy-start.1
  5.6 1.5 %collective-permute-start = (bf16[8,8,4224]{2,1,0:T(8,128)(2,1)S(1)}, bf16[8,8,4224]{2,1,0:T(8,128)(2,1)S(1)}, u32[]{:S(2)}, u32[]{:S(2)}) collective-permute-start(bf16[8,8,4224]{2,1,0:T(8,128)(2,1)S(1)} %get-tuple-element.37), channel_id=1, source_target_pairs={{0,1},{1,0},{2,3},{3,2},{4,5},{5,4},{6,7},{7,6},{8,9},{9,8},{10,11... | collective-permute-start | bytes 1622024 | tf_op jit(solution)/shard_map/ppermute | solution.py:414
  7.1 1.6 %collective-permute-done.recv_ref = bf16[8,8,4224]{2,1,0:T(8,128)(2,1)S(1)} collective-permute-done((bf16[8,8,4224]{2,1,0:T(8,128)(2,1)S(1)}, bf16[8,8,4224]{2,1,0:T(8,128)(2,1)S(1)}, u32[]{:S(2)}, u32[]{:S(2)}) %collective-permute-start) | collective-permute-done | bytes 540704 | tf_op jit(solution)/shard_map/ppermute | solution.py:414
  8.6 0.3 merge_cores.1
  9.0 19.2 %all_to_all.25.in_ref = bf16[8,8,4224]{2,1,0:T(8,128)(2,1)S(1)} all-to-all(bf16[8,8,4224]{2,1,0:T(8,128)(2,1)S(1)} %merge_cores.1), channel_id=1, replica_groups=mesh['seq_0'=2,'seq_1'=4,'exp_0'=2,'exp_1'=4,'exp_2'=2] {'exp_0','exp_1'}, dimensions={0} | all-to-all | bytes 1081344 | tf_op jit(solution)/shard_map/all_to_all | solution.py:410
  28.2 0.3 merge_column.1
  28.4 13.2 %all_to_all.26.in_ref = bf16[8,8,4224]{2,1,0:T(8,128)(2,1)S(1)} all-to-all(bf16[8,8,4224]{2,1,0:T(8,128)(2,1)S(1)} %merge_column.1), channel_id=1, replica_groups=mesh['seq_0'=2,'seq_1'=4,'exp_0'=2,'exp_1'=4,'exp_2'=2] {'seq_0','seq_1'}, dimensions={0} | all-to-all | bytes 1081344 | tf_op jit(solution)/shard_map/all_to_all | solution.py:410
  41.7 0.0 copy-done
  41.7 0.0 copy-done.1
  41.7 2.0 %experts.1 = (bf16[8,32,1024]{2,1,0:T(8,128)(2,1)S(1)}, bf16[16,1024]{1,0:T(8,128)(2,1)S(1)}, bf16[16,1024]{1,0:T(8,128)(2,1)S(1)}, bf16[16,512]{1,0:T(8,128)(2,...) custom-call(bf16[8,8,4224]{2,1,0:T(8,128)(2,1)S(1)} %all_to_all.26.in_ref, ...), custom_call_target="tpu_custom_call" | custom-call | tf_op jit(solution)/shard_map/experts/pallas_call | solution.py:245
  43.6 10.4 %all_to_all.27.in_ref = bf16[8,32,1024]{2,1,0:T(8,128)(2,1)S(1)} all-to-all(bf16[8,32,1024]{2,1,0:T(8,128)(2,1)S(1)} %get-tuple-element.38), channel_id=1, replica_groups=mesh['seq_0'=2,'seq_1'=4,'exp_0'=2,'exp_1'=4,'exp_2'=2] {'seq_0','seq_1'}, dimensions={0} | all-to-all | bytes 1048576 | tf_op jit(solution)/shard_map/all_to_all | solution.py:410
  54.0 0.1 slot_results.1
  54.2 11.8 %all_to_all.28.mine_ref = bf16[8,8,4224]{2,1,0:T(8,128)(2,1)S(1)} all-to-all(bf16[8,8,4224]{2,1,0:T(8,128)(2,1)S(1)} %slot_results.1), channel_id=1, replica_groups=mesh['seq_0'=2,'seq_1'=4,'exp_0'=2,'exp_1'=4,'exp_2'=2] {'exp_0','exp_1'}, dimensions={0} | all-to-all | bytes 1081344 | tf_op jit(solution)/shard_map/all_to_all | solution.py:410
  66.0 4.5 %collective-permute-start.1 = (bf16[8,8,4224]{2,1,0:T(8,128)(2,1)S(1)}, bf16[8,8,4224]{2,1,0:T(8,128)(2,1)S(1)}, u32[]{:S(2)}, u32[]{:S(2)}) collective-permute-start(bf16[8,8,4224]{2,1,0:T(8,128)(2,1)S(1)} %all_to_all.28.mine_ref), channel_id=1, source_target_pairs={{0,1},{1,0},{2,3},{3,2},{4,5},{5,4},{6,7},{7,6},{8,9},{9,8},{10,11... | collective-permute-start | bytes 1622024 | tf_op jit(solution)/shard_map/ppermute | solution.py:414
  70.5 1.6 %collective-permute-done.1.other_ref = bf16[8,8,4224]{2,1,0:T(8,128)(2,1)S(1)} collective-permute-done((bf16[8,8,4224]{2,1,0:T(8,128)(2,1)S(1)}, bf16[8,8,4224]{2,1,0:T(8,128)(2,1)S(1)}, u32[]{:S(2)}, u32[]{:S(2)}) %collective-permute-start.1) | collective-permute-done | bytes 540704 | tf_op jit(solution)/shard_map/ppermute | solution.py:414
  72.0 3.6 %second_pass.1 = (bf16[2,128,1024]{2,1,0:T(8,128)(2,1)S(1)}, bf16[2,256,1024]{2,1,0:T(8,128)(2,1)S(1)}, bf16[2,256,768]{2,1,0:T(8,128)(2,1)S(1)}, bf16[1024,128]{1,0:T(8,128)(2,1)}) custom-call(bf16[2,768,1024]{2,1,0:T(8,128)(2,1)S(1)} %get-tuple-element.30.tok_ref, bf16[2,768,1024]{2,1,0:T(8,128)(2,1)S(1)} %get-tuple-element.31.grad_ref, ...), custom_call_target="tpu_custom_call" | custom-call | tf_op jit(solution)/shard_map/second_pass/pallas_call | solution.py:361
  75.7 3.8 %all-to-all-start.4 = ((bf16[128,8,128]{2,1,0:T(8,128)(2,1)}), bf16[128,8,128]{2,1,0:T(8,128)(2,1)S(1)}, u32[]{:S(2)}, u32[]{:S(2)}) async-start(bf16[128,8,128]{2,1,0:T(8,128)(2,1)} %bitcast), calls=%async_computation.4 | async-start | bytes 524288 | tf_op jit(solution)/shard_map/all_to_all | solution.py:410
  79.4 2.6 %weight_grads.1 = (bf16[2,1024,512]{2,1,0:T(8,128)(2,1)}, bf16[2,512,1024]{2,1,0:T(8,128)(2,1)}) custom-call(bf16[16,1024]{1,0:T(8,128)(2,1)S(1)} %get-tuple-element.47.rows_ref, bf16[16,1024]{1,0:T(8,128)(2,1)S(1)} %get-tuple-element.48.grads_ref, bf16[16,512]{1,0:T(8,128)(2,1)S(1)} %get-tuple-element.49.hidden_ref, ...), custom_call_target="tpu_custom_call" | custom-call | flops 67108864 | bytes 4194304 | tf_op jit(solution)/shard_map/weight_grads/pallas_call | solution.py:277
  82.0 4.4 %token_outputs.1 = (bf16[2,768,1024]{2,1,0:T(8,128)(2,1)}, bf16[2,768,1024]{2,1,0:T(8,128)(2,1)}) custom-call(bf16[2,128,768]{2,1,0:T(8,128)(2,1)S(1)} %get-tuple-element.29.mix_ref, bf16[2,256,768]{2,1,0:T(8,128)(2,1)S(1)} %get-tuple-element.41.weights_ref, bf16[2,128,1024]{2,1,0:T(8,128)(2,1)S(1)} %get-tuple-element.42.outs_ref, ...), custom_call_target="tpu_custom_call" | custom-call | flops 1207959552 | bytes 9437184 | tf_op jit(solution)/shard_map/token_outputs/pallas_call | solution.py:382
  86.4 4.1 %all-to-all-done.4 = bf16[128,8,128]{2,1,0:T(8,128)(2,1)S(1)} async-done(((bf16[128,8,128]{2,1,0:T(8,128)(2,1)}), bf16[128,8,128]{2,1,0:T(8,128)(2,1)S(1)}, u32[]{:S(2)}, u32[]{:S(2)}) %all-to-all-start.4) | async-done | bytes 262176 | tf_op jit(solution)/shard_map/all_to_all | solution.py:410
  90.5 0.7 add_up.1
Async XLA Ops:
  5.6 36.1 %copy-start = (bf16[2,1024,512]{2,1,0:T(8,128)(2,1)S(1)}, bf16[2,1024,512]{2,1,0:T(8,128)(2,1)}, u32[]{:S(2)}) copy-start(bf16[2,1024,512]{2,1,0:T(8,128)(2,1)} %w_in_ref.1) | copy-start | bytes 6291460
  5.6 36.1 %copy-start.1 = (bf16[2,512,1024]{2,1,0:T(8,128)(2,1)S(1)}, bf16[2,512,1024]{2,1,0:T(8,128)(2,1)}, u32[]{:S(2)}) copy-start(bf16[2,512,1024]{2,1,0:T(8,128)(2,1)} %w_out_ref.1) | copy-start | bytes 6291460
  5.6 3.1 %collective-permute-start = (bf16[8,8,4224]{2,1,0:T(8,128)(2,1)S(1)}, bf16[8,8,4224]{2,1,0:T(8,128)(2,1)S(1)}, u32[]{:S(2)}, u32[]{:S(2)}) collective-permute-start(bf16[8,8,4224]{2,1,0:T(8,128)(2,1)S(1)} %get-tuple-element.37), channel_id=1, source_target_pairs={{0,1},{1,0},{2,3},{3,2},{4,5},{5,4},{6,7},{7,6},{8,9},{9,8},{10,11... | collective-permute-start | bytes 1622024 | tf_op jit(solution)/shard_map/ppermute | solution.py:414
  66.0 6.1 %collective-permute-start.1 = (bf16[8,8,4224]{2,1,0:T(8,128)(2,1)S(1)}, bf16[8,8,4224]{2,1,0:T(8,128)(2,1)S(1)}, u32[]{:S(2)}, u32[]{:S(2)}) collective-permute-start(bf16[8,8,4224]{2,1,0:T(8,128)(2,1)S(1)} %all_to_all.28.mine_ref), channel_id=1, source_target_pairs={{0,1},{1,0},{2,3},{3,2},{4,5},{5,4},{6,7},{7,6},{8,9},{9,8},{10,11... | collective-permute-start | bytes 1622024 | tf_op jit(solution)/shard_map/ppermute | solution.py:414
  75.7 14.8 %all-to-all-start.4 = ((bf16[128,8,128]{2,1,0:T(8,128)(2,1)}), bf16[128,8,128]{2,1,0:T(8,128)(2,1)S(1)}, u32[]{:S(2)}, u32[]{:S(2)}) async-start(bf16[128,8,128]{2,1,0:T(8,128)(2,1)} %bitcast), calls=%async_computation.4 | async-start | bytes 524288 | tf_op jit(solution)/shard_map/all_to_all | solution.py:410

commit v3 on v2

--- a/solution.py
+++ b/solution.py
@@ -58,12 +58,12 @@
 def mixing_of(logits_t):
     peak = jnp.max(logits_t, axis=0, keepdims=True)
     terms = jnp.exp(logits_t - peak)
-    return terms / jnp.sum(terms, axis=0, keepdims=True)
+    return terms * (1.0 / jnp.sum(terms, axis=0, keepdims=True))
 
 
 def first_pass(
     tok_hbm, router_hbm, grad_hbm,
-    tok_ref, grad_ref, router_t_ref, terms_ref, mixing_ref, mix_ref, stats_ref, keep_ref, send_ref,
+    tok_ref, tok_t_ref, grad_ref, router_t_ref, terms_ref, mixing_ref, mix_ref, stats_ref, keep_ref, send_ref,
     router_buf, router_f, sems,
 ):
     core = lax.axis_index(CORE)
@@ -87,7 +87,10 @@
     columns = [None] * 6
     for c in range(clips):
         copies[1 + c].wait()
-        logits_t = dot_nt(router_t_ref[...], tok_ref[c])
+        tok_t_ref[:, pl.ds(c * rows, rows)] = tok_ref[c].T
+    both = dot_nn(router_t_ref[...], tok_t_ref[...])
+    for c in range(clips):
+        logits_t = both[:, c * rows : (c + 1) * rows]
         peak = jnp.max(logits_t, axis=1, keepdims=True).astype(BF16).astype(F32)
         terms = jnp.exp(logits_t - peak)
         terms_ref[c] = terms
@@ -102,6 +105,8 @@
             at = pl.ds(c * width, width)
             keep_ref[q, :, at] = sums[q * GROUP : (q + 1) * GROUP]
             send_ref[q, :, at] = sums[half + q * GROUP : half + (q + 1) * GROUP]
+    for c in range(clips):
+        copies[1 + clips + c].wait()
     stats = packed(columns)
     stats_ref[...] = stats
     stats = stats.astype(BF16)
@@ -110,7 +115,6 @@
         keep_ref[q, :, at] = stats[q * GROUP : (q + 1) * GROUP]
         send_ref[q, :, at] = stats[half + q * GROUP : half + (q + 1) * GROUP]
     for c in range(clips):
-        copies[1 + clips + c].wait()
         sums = dot_nn(mix_ref[c], grad_ref[c]).astype(BF16)
         for q in range(keep_ref.shape[0]):
             at = pl.ds((2 + c) * width, width)
@@ -129,6 +133,7 @@
     groups = slots // GROUP // 2
     shapes = [
         (tokens.shape, BF16),
+        ((width, clips * rows), BF16),
         (grad_out.shape, BF16),
         ((slots, width), BF16),
         ((clips, slots, rows), F32),
@@ -311,7 +316,7 @@
 
 
 def second_pass(
-    tok_ref, grad_ref, terms_ref, mixing_ref, local_ref, router_t_ref, mine_ref, other_ref,
+    tok_ref, tok_t_ref, grad_ref, terms_ref, mixing_ref, local_ref, router_t_ref, mine_ref, other_ref,
     outs_ref, backs_ref, weights_ref, part_ref, ordered,
 ):
     core = lax.axis_index(CORE)
@@ -338,7 +343,7 @@
         dispatch = terms_ref[c] * scale
         weights_ref[c, pl.ds(0, slots), :] = dispatch.astype(BF16)
         mixing = mixing_ref[c]
-        dispatch_grad = dot_nt(backs_ref[c, pl.ds(0, slots), :], tok_ref[c])
+        dispatch_grad = dot_nn(backs_ref[c, pl.ds(0, slots), :], tok_t_ref[:, pl.ds(c * rows, rows)])
         mixing_grad = dot_nt(outs_ref[c], grad_ref[c])
         logit_grad = dispatch * (dispatch_grad - inner) + mixing * (
             mixing_grad - jnp.sum(mixing * mixing_grad, axis=0, keepdims=True)
@@ -354,19 +359,19 @@
     part_ref[...] = ordered[...].T.astype(BF16)
 
 
-def run_second_pass(tok, grad, terms, mixing, local, router_t, mine, other):
+def run_second_pass(tok, tok_t, grad, terms, mixing, local, router_t, mine, other):
     clips, rows, width = tok.shape
     slots = router_t.shape[0]
     shapes = [(clips, slots, width), (clips, 2 * slots, width), (clips, 2 * slots, rows), (width, slots)]
     return pl.pallas_call(
         second_pass,
-        in_specs=[VMEM] * 8,
+        in_specs=[VMEM] * 9,
         out_specs=[VMEM] * len(shapes),
         out_shape=[jax.ShapeDtypeStruct(shape, BF16) for shape in shapes],
         scratch_shapes=[pltpu.VMEM((slots, width), F32)],
         compiler_params=params(28),
         name="second_pass",
-    )(tok, grad, terms, mixing, local, router_t, mine, other)
+    )(tok, tok_t, grad, terms, mixing, local, router_t, mine, other)
 
 
 def token_outputs(mix_ref, weights_ref, outs_ref, backs_ref, mixed_ref, grad_tokens_ref):
@@ -419,7 +424,7 @@
     width = tokens.shape[2]
     row = 4 * width + LANES
     chips = lax.axis_size(CHIPS_EXP)
-    tok, grad, router_t, terms, mixing, mix, local, keep, send = run_first_pass(tokens, router, grad_out)
+    tok, tok_t, grad, router_t, terms, mixing, mix, local, keep, send = run_first_pass(tokens, router, grad_out)
     recv = swapped(send)
     small = params(16)
     halves = pl.pallas_call(
@@ -436,7 +441,7 @@
     )(arrived, slot_in, stats)
     mine = exchanged(results, CHIPS_EXP)
     other = swapped(mine)
-    outs, backs, weights, part = run_second_pass(tok, grad, terms, mixing, local, router_t, mine, other)
+    outs, backs, weights, part = run_second_pass(tok, tok_t, grad, terms, mixing, local, router_t, mine, other)
     devices = lax.axis_size(SEQ_EXP)
     arrived = exchanged(part.reshape(devices, width // devices, part.shape[1]), SEQ_EXP)
     mixed, grad_tokens = run_token_outputs(mix, weights, outs, backs)

time: 91.5 us -> 90.3 us (0.987)
  Pallas kernels: 18.9 us -> 17.7 us
    pallas_call x1, Pallas kernels: 4.93 us -> 3.98 us  [run_first_pass(): pl.pallas_call(first_pass, in_specs=[HBM] * 3, out_specs=[VMEM] * len(sha...]
where the time goes in v3:
time: 90.3 us; the launch traced here: 90 us
  blocking collectives  54.6 us (60%)
  Pallas kernels  17.7 us (20%)
  starting transfers between devices  9.75 us (11%)
  waiting for transfers between devices  7.2 us (8%)
    all_to_all x4, blocking collectives, exchanged(): return lax.all_to_all(array, axes, split_axis=0, concat_axis=0, tiled=True)  54.6 us
    ppermute x2, starting transfers between devices, swapped(): return lax.ppermute(array, CORE, [(0, 1), (1, 0)])  5.99 us
    pallas_call x1, Pallas kernels, run_token_outputs(): pl.pallas_call(token_outputs, grid=(clips, rows // block), in_specs=[pl.B...  4.42 us
    all_to_all x1, waiting for transfers between devices, exchanged(): return lax.all_to_all(array, axes, split_axis=0, concat_axis=0, tiled=True)  4.08 us
    pallas_call x1, Pallas kernels, run_first_pass(): pl.pallas_call(first_pass, in_specs=[HBM] * 3, out_specs=[VMEM] * len(sha...  3.98 us
    all_to_all x1, starting transfers between devices, exchanged(): return lax.all_to_all(array, axes, split_axis=0, concat_axis=0, tiled=True)  3.75 us
    pallas_call x1, Pallas kernels, run_second_pass(): pl.pallas_call(second_pass, in_specs=[VMEM] * 9, out_specs=[VMEM] * len(s...  3.37 us
    ppermute x2, waiting for transfers between devices, swapped(): return lax.ppermute(array, CORE, [(0, 1), (1, 0)])  3.12 us
  transfers between devices with their start and end apart: 3, of which 3 were waited for; matrix products, arithmetic and copies ran while one was open for 0% of the time, Pallas kernels for 8%

profile of v3, /device:TPU:1, one launch (start us, length us, event | category | flops | bytes accessed | tf_op | source)
XLA Modules:
  0.0 90.0 jit_solution(18130568532330351749)
XLA Ops:
  0.6 4.0 %first_pass.1 = (bf16[2,768,1024]{2,1,0:T(8,128)(2,1)S(1)}, bf16[1024,1536]{1,0:T(8,128)(2,1)S(1)}, bf16[2,768,1024]{2,1,0:T(8,128)(2,1)S(1)}, bf16[128,1024]{1,...) custom-call(bf16[2,768,1024]{2,1,0:T(8,128)(2,1)} %tok_hbm.1, ...), custom_call_target="tpu_custom_call" | custom-call | tf_op jit(solution)/shard_map/first_pass/pallas_call | solution.py:146
  4.6 0.0 copy-start
  4.6 0.0 copy-start.1
  4.6 1.5 %collective-permute-start = (bf16[8,8,4224]{2,1,0:T(8,128)(2,1)S(1)}, bf16[8,8,4224]{2,1,0:T(8,128)(2,1)S(1)}, u32[]{:S(2)}, u32[]{:S(2)}) collective-permute-start(bf16[8,8,4224]{2,1,0:T(8,128)(2,1)S(1)} %get-tuple-element.39), channel_id=1, source_target_pairs={{0,1},{1,0},{2,3},{3,2},{4,5},{5,4},{6,7},{7,6},{8,9},{9,8},{10,11... | collective-permute-start | bytes 1622024 | tf_op jit(solution)/shard_map/ppermute | solution.py:419
  6.1 1.6 %collective-permute-done.recv_ref = bf16[8,8,4224]{2,1,0:T(8,128)(2,1)S(1)} collective-permute-done((bf16[8,8,4224]{2,1,0:T(8,128)(2,1)S(1)}, bf16[8,8,4224]{2,1,0:T(8,128)(2,1)S(1)}, u32[]{:S(2)}, u32[]{:S(2)}) %collective-permute-start) | collective-permute-done | bytes 540704 | tf_op jit(solution)/shard_map/ppermute | solution.py:419
  7.7 0.3 merge_cores.1
  8.0 19.2 %all_to_all.25.in_ref = bf16[8,8,4224]{2,1,0:T(8,128)(2,1)S(1)} all-to-all(bf16[8,8,4224]{2,1,0:T(8,128)(2,1)S(1)} %merge_cores.1), channel_id=1, replica_groups=mesh['seq_0'=2,'seq_1'=4,'exp_0'=2,'exp_1'=4,'exp_2'=2] {'exp_0','exp_1'}, dimensions={0} | all-to-all | bytes 1081344 | tf_op jit(solution)/shard_map/all_to_all | solution.py:415
  27.2 0.3 merge_column.1
  27.5 13.2 %all_to_all.26.in_ref = bf16[8,8,4224]{2,1,0:T(8,128)(2,1)S(1)} all-to-all(bf16[8,8,4224]{2,1,0:T(8,128)(2,1)S(1)} %merge_column.1), channel_id=1, replica_groups=mesh['seq_0'=2,'seq_1'=4,'exp_0'=2,'exp_1'=4,'exp_2'=2] {'seq_0','seq_1'}, dimensions={0} | all-to-all | bytes 1081344 | tf_op jit(solution)/shard_map/all_to_all | solution.py:415
  40.7 0.0 copy-done
  40.7 0.0 copy-done.1
  40.7 2.0 %experts.1 = (bf16[8,32,1024]{2,1,0:T(8,128)(2,1)S(1)}, bf16[16,1024]{1,0:T(8,128)(2,1)S(1)}, bf16[16,1024]{1,0:T(8,128)(2,1)S(1)}, bf16[16,512]{1,0:T(8,128)(2,...) custom-call(bf16[8,8,4224]{2,1,0:T(8,128)(2,1)S(1)} %all_to_all.26.in_ref, ...), custom_call_target="tpu_custom_call" | custom-call | tf_op jit(solution)/shard_map/experts/pallas_call | solution.py:250
  42.7 10.4 %all_to_all.27.in_ref = bf16[8,32,1024]{2,1,0:T(8,128)(2,1)S(1)} all-to-all(bf16[8,32,1024]{2,1,0:T(8,128)(2,1)S(1)} %get-tuple-element.40), channel_id=1, replica_groups=mesh['seq_0'=2,'seq_1'=4,'exp_0'=2,'exp_1'=4,'exp_2'=2] {'seq_0','seq_1'}, dimensions={0} | all-to-all | bytes 1048576 | tf_op jit(solution)/shard_map/all_to_all | solution.py:415
  53.1 0.1 slot_results.1
  53.2 11.8 %all_to_all.28.mine_ref = bf16[8,8,4224]{2,1,0:T(8,128)(2,1)S(1)} all-to-all(bf16[8,8,4224]{2,1,0:T(8,128)(2,1)S(1)} %slot_results.1), channel_id=1, replica_groups=mesh['seq_0'=2,'seq_1'=4,'exp_0'=2,'exp_1'=4,'exp_2'=2] {'exp_0','exp_1'}, dimensions={0} | all-to-all | bytes 1081344 | tf_op jit(solution)/shard_map/all_to_all | solution.py:415
  65.0 4.5 %collective-permute-start.1 = (bf16[8,8,4224]{2,1,0:T(8,128)(2,1)S(1)}, bf16[8,8,4224]{2,1,0:T(8,128)(2,1)S(1)}, u32[]{:S(2)}, u32[]{:S(2)}) collective-permute-start(bf16[8,8,4224]{2,1,0:T(8,128)(2,1)S(1)} %all_to_all.28.mine_ref), channel_id=1, source_target_pairs={{0,1},{1,0},{2,3},{3,2},{4,5},{5,4},{6,7},{7,6},{8,9},{9,8},{10,11... | collective-permute-start | bytes 1622024 | tf_op jit(solution)/shard_map/ppermute | solution.py:419
  69.5 1.6 %collective-permute-done.1.other_ref = bf16[8,8,4224]{2,1,0:T(8,128)(2,1)S(1)} collective-permute-done((bf16[8,8,4224]{2,1,0:T(8,128)(2,1)S(1)}, bf16[8,8,4224]{2,1,0:T(8,128)(2,1)S(1)}, u32[]{:S(2)}, u32[]{:S(2)}) %collective-permute-start.1) | collective-permute-done | bytes 540704 | tf_op jit(solution)/shard_map/ppermute | solution.py:419
  71.1 3.4 %second_pass.1 = (bf16[2,128,1024]{2,1,0:T(8,128)(2,1)S(1)}, bf16[2,256,1024]{2,1,0:T(8,128)(2,1)S(1)}, bf16[2,256,768]{2,1,0:T(8,128)(2,1)S(1)}, bf16[1024,128]{1,0:T(8,128)(2,1)}) custom-call(bf16[2,768,1024]{2,1,0:T(8,128)(2,1)S(1)} %get-tuple-element.31.tok_ref, bf16[1024,1536]{1,0:T(8,128)(2,1)S(1)} %get-tuple-element.32.tok_t_ref, ...), custom_call_target="tpu_custom_call" | custom-call | tf_op jit(solution)/shard_map/second_pass/pallas_call | solution.py:366
  74.4 3.8 %all-to-all-start.4 = ((bf16[128,8,128]{2,1,0:T(8,128)(2,1)}), bf16[128,8,128]{2,1,0:T(8,128)(2,1)S(1)}, u32[]{:S(2)}, u32[]{:S(2)}) async-start(bf16[128,8,128]{2,1,0:T(8,128)(2,1)} %bitcast), calls=%async_computation.4 | async-start | bytes 524288 | tf_op jit(solution)/shard_map/all_to_all | solution.py:415
  78.2 2.6 %weight_grads.1 = (bf16[2,1024,512]{2,1,0:T(8,128)(2,1)}, bf16[2,512,1024]{2,1,0:T(8,128)(2,1)}) custom-call(bf16[16,1024]{1,0:T(8,128)(2,1)S(1)} %get-tuple-element.49.rows_ref, bf16[16,1024]{1,0:T(8,128)(2,1)S(1)} %get-tuple-element.50.grads_ref, bf16[16,512]{1,0:T(8,128)(2,1)S(1)} %get-tuple-element.51.hidden_ref, ...), custom_call_target="tpu_custom_call" | custom-call | flops 67108864 | bytes 4194304 | tf_op jit(solution)/shard_map/weight_grads/pallas_call | solution.py:282
  80.8 4.4 %token_outputs.1 = (bf16[2,768,1024]{2,1,0:T(8,128)(2,1)}, bf16[2,768,1024]{2,1,0:T(8,128)(2,1)}) custom-call(bf16[2,128,768]{2,1,0:T(8,128)(2,1)S(1)} %get-tuple-element.30.mix_ref, bf16[2,256,768]{2,1,0:T(8,128)(2,1)S(1)} %get-tuple-element.43.weights_ref, bf16[2,128,1024]{2,1,0:T(8,128)(2,1)S(1)} %get-tuple-element.44.outs_ref, ...), custom_call_target="tpu_custom_call" | custom-call | flops 1207959552 | bytes 9437184 | tf_op jit(solution)/shard_map/token_outputs/pallas_call | solution.py:387
  85.2 4.1 %all-to-all-done.4 = bf16[128,8,128]{2,1,0:T(8,128)(2,1)S(1)} async-done(((bf16[128,8,128]{2,1,0:T(8,128)(2,1)}), bf16[128,8,128]{2,1,0:T(8,128)(2,1)S(1)}, u32[]{:S(2)}, u32[]{:S(2)}) %all-to-all-start.4) | async-done | bytes 262176 | tf_op jit(solution)/shard_map/all_to_all | solution.py:415
  89.3 0.7 add_up.1
Async XLA Ops:
  4.6 36.1 %copy-start = (bf16[2,1024,512]{2,1,0:T(8,128)(2,1)S(1)}, bf16[2,1024,512]{2,1,0:T(8,128)(2,1)}, u32[]{:S(2)}) copy-start(bf16[2,1024,512]{2,1,0:T(8,128)(2,1)} %w_in_ref.1) | copy-start | bytes 6291460
  4.6 36.1 %copy-start.1 = (bf16[2,512,1024]{2,1,0:T(8,128)(2,1)S(1)}, bf16[2,512,1024]{2,1,0:T(8,128)(2,1)}, u32[]{:S(2)}) copy-start(bf16[2,512,1024]{2,1,0:T(8,128)(2,1)} %w_out_ref.1) | copy-start | bytes 6291460
  4.6 3.1 %collective-permute-start = (bf16[8,8,4224]{2,1,0:T(8,128)(2,1)S(1)}, bf16[8,8,4224]{2,1,0:T(8,128)(2,1)S(1)}, u32[]{:S(2)}, u32[]{:S(2)}) collective-permute-start(bf16[8,8,4224]{2,1,0:T(8,128)(2,1)S(1)} %get-tuple-element.39), channel_id=1, source_target_pairs={{0,1},{1,0},{2,3},{3,2},{4,5},{5,4},{6,7},{7,6},{8,9},{9,8},{10,11... | collective-permute-start | bytes 1622024 | tf_op jit(solution)/shard_map/ppermute | solution.py:419
  65.0 6.1 %collective-permute-start.1 = (bf16[8,8,4224]{2,1,0:T(8,128)(2,1)S(1)}, bf16[8,8,4224]{2,1,0:T(8,128)(2,1)S(1)}, u32[]{:S(2)}, u32[]{:S(2)}) collective-permute-start(bf16[8,8,4224]{2,1,0:T(8,128)(2,1)S(1)} %all_to_all.28.mine_ref), channel_id=1, source_target_pairs={{0,1},{1,0},{2,3},{3,2},{4,5},{5,4},{6,7},{7,6},{8,9},{9,8},{10,11... | collective-permute-start | bytes 1622024 | tf_op jit(solution)/shard_map/ppermute | solution.py:419
  74.4 14.8 %all-to-all-start.4 = ((bf16[128,8,128]{2,1,0:T(8,128)(2,1)}), bf16[128,8,128]{2,1,0:T(8,128)(2,1)S(1)}, u32[]{:S(2)}, u32[]{:S(2)}) async-start(bf16[128,8,128]{2,1,0:T(8,128)(2,1)} %bitcast), calls=%async_computation.4 | async-start | bytes 524288 | tf_op jit(solution)/shard_map/all_to_all | solution.py:415

commit v4 on v3

--- a/solution.py
+++ b/solution.py
@@ -315,36 +315,72 @@
         out_ref[q, :, pl.ds(4 * width, LANES)] = tile.astype(BF16)
 
 
+def turn(in_ref, out_ref):
+    rows = in_ref.shape[1]
+    for c in range(in_ref.shape[0]):
+        out_ref[:, pl.ds(c * rows, rows)] = in_ref[c].T
+
+
+def half_products(tok_t_ref, grad_t_ref, slots_ref, outs_ref, backs_ref, stats_ref, dispatch_grad_ref, mixing_grad_ref):
+    clips, rows = outs_ref.shape[0], dispatch_grad_ref.shape[2]
+    width = outs_ref.shape[2]
+    for q in range(slots_ref.shape[0]):
+        at = pl.ds(q * GROUP, GROUP)
+        for c in range(clips):
+            outs_ref[c, at, :] = slots_ref[q, :, pl.ds(c * width, width)]
+            backs_ref[c, at, :] = slots_ref[q, :, pl.ds((2 + c) * width, width)]
+        stats_ref[at, :] = slots_ref[q, :, pl.ds(4 * width, LANES)].astype(F32)
+    for c in range(clips):
+        at = pl.ds(c * rows, rows)
+        dispatch_grad_ref[c] = dot_nn(backs_ref[c], tok_t_ref[:, at])
+        mixing_grad_ref[c] = dot_nn(outs_ref[c], grad_t_ref[:, at])
+
+
+def run_half_products(tok_t, grad_t, slots, clips):
+    half, width = slots.shape[0] * GROUP, tok_t.shape[0]
+    rows = tok_t.shape[1] // clips
+    shapes = [
+        ((clips, half, width), BF16),
+        ((clips, half, width), BF16),
+        ((half, LANES), F32),
+        ((clips, half, rows), F32),
+        ((clips, half, rows), F32),
+    ]
+    return pl.pallas_call(
+        half_products,
+        in_specs=[VMEM] * 3,
+        out_specs=[VMEM] * len(shapes),
+        out_shape=[jax.ShapeDtypeStruct(*shape) for shape in shapes],
+        compiler_params=params(16),
+        name="half_products",
+    )(tok_t, grad_t, slots)
+
+
 def second_pass(
-    tok_ref, tok_t_ref, grad_ref, terms_ref, mixing_ref, local_ref, router_t_ref, mine_ref, other_ref,
-    outs_ref, backs_ref, weights_ref, part_ref, ordered,
+    tok_ref, tok_t_ref, grad_t_ref, terms_ref, mixing_ref, local_ref,
+    own_stats_ref, own_dispatch_ref, own_mixing_ref, slots_ref,
+    outs_ref, backs_ref, weights_ref, part_ref, stats_ref, other_dispatch_ref, other_mixing_ref, ordered,
 ):
     core = lax.axis_index(CORE)
     clips, rows, width = tok_ref.shape
-    slots = router_t_ref.shape[0]
+    slots = terms_ref.shape[1]
     half = slots // 2
-    tiles = []
-    for k, ref in enumerate((mine_ref, other_ref)):
-        for q in range(ref.shape[0]):
-            at = pl.ds(k * half + q * GROUP, GROUP)
-            for c in range(clips):
-                outs_ref[c, at, :] = ref[q, :, pl.ds(c * width, width)]
-                backs_ref[c, at, :] = ref[q, :, pl.ds((2 + c) * width, width)]
-            tiles.append(ref[q, :, pl.ds(4 * width, LANES)].astype(F32))
-    tile = jnp.concatenate(tiles, axis=0)
+    half_products(
+        tok_t_ref, grad_t_ref, slots_ref, outs_ref, backs_ref, stats_ref, other_dispatch_ref, other_mixing_ref
+    )
+    tile = jnp.concatenate([own_stats_ref[...], stats_ref[...]], axis=0)
     local = local_ref[...]
     column = lambda k: tile[:, k : k + 1]
     total = jnp.zeros((slots, width), F32)
     for c in range(clips):
-        backs_ref[c, pl.ds(slots, slots), :] = router_t_ref[...]
         mass = column(2 + 3 * c) + column(3 + 3 * c) + column(4 + 3 * c)
         inner = column(8 + 3 * c) + column(9 + 3 * c) + column(10 + 3 * c)
         scale = jnp.exp(local[:, c : c + 1] - column(c)) / mass
         dispatch = terms_ref[c] * scale
         weights_ref[c, pl.ds(0, slots), :] = dispatch.astype(BF16)
         mixing = mixing_ref[c]
-        dispatch_grad = dot_nn(backs_ref[c, pl.ds(0, slots), :], tok_t_ref[:, pl.ds(c * rows, rows)])
-        mixing_grad = dot_nt(outs_ref[c], grad_ref[c])
+        dispatch_grad = jnp.concatenate([own_dispatch_ref[c], other_dispatch_ref[c]], axis=0)
+        mixing_grad = jnp.concatenate([own_mixing_ref[c], other_mixing_ref[c]], axis=0)
         logit_grad = dispatch * (dispatch_grad - inner) + mixing * (
             mixing_grad - jnp.sum(mixing * mixing_grad, axis=0, keepdims=True)
         )
@@ -359,39 +395,53 @@
     part_ref[...] = ordered[...].T.astype(BF16)
 
 
-def run_second_pass(tok, tok_t, grad, terms, mixing, local, router_t, mine, other):
+def run_second_pass(tok, tok_t, grad_t, terms, mixing, local, own, other):
     clips, rows, width = tok.shape
-    slots = router_t.shape[0]
-    shapes = [(clips, slots, width), (clips, 2 * slots, width), (clips, 2 * slots, rows), (width, slots)]
+    slots = terms.shape[1]
+    shapes = [(clips, slots // 2, width), (clips, slots // 2, width), (clips, 2 * slots, rows), (width, slots)]
     return pl.pallas_call(
         second_pass,
-        in_specs=[VMEM] * 9,
+        in_specs=[VMEM] * 10,
         out_specs=[VMEM] * len(shapes),
         out_shape=[jax.ShapeDtypeStruct(shape, BF16) for shape in shapes],
-        scratch_shapes=[pltpu.VMEM((slots, width), F32)],
-        compiler_params=params(28),
+        scratch_shapes=[
+            pltpu.VMEM((slots // 2, LANES), F32),
+            pltpu.VMEM((clips, slots // 2, rows), F32),
+            pltpu.VMEM((clips, slots // 2, rows), F32),
+            pltpu.VMEM((slots, width), F32),
+        ],
+        compiler_params=params(24),
         name="second_pass",
-    )(tok, tok_t, grad, terms, mixing, local, router_t, mine, other)
-
-
-def token_outputs(mix_ref, weights_ref, outs_ref, backs_ref, mixed_ref, grad_tokens_ref):
-    mixed_ref[0] = dot_tn(mix_ref[0], outs_ref[0]).astype(BF16)
-    grad_tokens_ref[0] = dot_tn(weights_ref[0], backs_ref[0]).astype(BF16)
-
-
-def run_token_outputs(mix, weights, outs, backs):
+    )(tok, tok_t, grad_t, terms, mixing, local, *own, other)
+
+
+def token_outputs(
+    mix_ref, weights_ref, own_outs_ref, other_outs_ref, own_backs_ref, other_backs_ref, router_t_ref,
+    mixed_ref, grad_tokens_ref,
+):
+    outs = jnp.concatenate([own_outs_ref[0], other_outs_ref[0]], axis=0)
+    backs = jnp.concatenate([own_backs_ref[0], other_backs_ref[0], router_t_ref[...]], axis=0)
+    mixed_ref[0] = dot_tn(mix_ref[0], outs).astype(BF16)
+    grad_tokens_ref[0] = dot_tn(weights_ref[0], backs).astype(BF16)
+
+
+def run_token_outputs(mix, weights, own_outs, other_outs, own_backs, other_backs, router_t):
     clips, slots, rows = mix.shape
-    width = outs.shape[2]
-    block = 256
+    width = own_outs.shape[2]
+    block = 384
     out = pl.BlockSpec((1, block, width), lambda c, t: (c, t, 0))
+    part = pl.BlockSpec((1, slots // 2, width), lambda c, t: (c, 0, 0))
     return pl.pallas_call(
         token_outputs,
         grid=(clips, rows // block),
         in_specs=[
             pl.BlockSpec((1, slots, block), lambda c, t: (c, 0, t)),
             pl.BlockSpec((1, 2 * slots, block), lambda c, t: (c, 0, t)),
-            pl.BlockSpec((1, slots, width), lambda c, t: (c, 0, 0)),
-            pl.BlockSpec((1, 2 * slots, width), lambda c, t: (c, 0, 0)),
+            part,
+            part,
+            part,
+            part,
+            pl.BlockSpec((slots, width), lambda c, t: (0, 0)),
         ],
         out_specs=[out, out],
         out_shape=[jax.ShapeDtypeStruct((clips, rows, width), BF16)] * 2,
@@ -400,7 +450,7 @@
             flops=6 * clips * rows * slots * width, transcendentals=0, bytes_accessed=6 * clips * rows * width
         ),
         name="token_outputs",
-    )(mix, weights, outs, backs)
+    )(mix, weights, own_outs, other_outs, own_backs, other_backs, router_t)
 
 
 def add_up(in_ref, out_ref):
@@ -427,6 +477,15 @@
     tok, tok_t, grad, router_t, terms, mixing, mix, local, keep, send = run_first_pass(tokens, router, grad_out)
     recv = swapped(send)
     small = params(16)
+    grad_t = pl.pallas_call(
+        turn,
+        in_specs=[VMEM],
+        out_specs=VMEM,
+        out_shape=jax.ShapeDtypeStruct(tok_t.shape, BF16),
+        compiler_params=small,
+        name="turn",
+    )(grad)
+    recv, grad_t = lax.optimization_barrier((recv, grad_t))
     halves = pl.pallas_call(
         merge_cores, out_shape=jax.ShapeDtypeStruct((chips, GROUP, row), BF16), compiler_params=small, name="merge_cores"
     )(keep, recv)
@@ -441,10 +500,12 @@
     )(arrived, slot_in, stats)
     mine = exchanged(results, CHIPS_EXP)
     other = swapped(mine)
-    outs, backs, weights, part = run_second_pass(tok, tok_t, grad, terms, mixing, local, router_t, mine, other)
+    own_outs, own_backs, *own = run_half_products(tok_t, grad_t, mine, tokens.shape[0])
+    other, *own = lax.optimization_barrier((other, *own))
+    other_outs, other_backs, weights, part = run_second_pass(tok, tok_t, grad_t, terms, mixing, local, own, other)
     devices = lax.axis_size(SEQ_EXP)
     arrived = exchanged(part.reshape(devices, width // devices, part.shape[1]), SEQ_EXP)
-    mixed, grad_tokens = run_token_outputs(mix, weights, outs, backs)
+    mixed, grad_tokens = run_token_outputs(mix, weights, own_outs, other_outs, own_backs, other_backs, router_t)
     grad_router = pl.pallas_call(
         add_up, out_shape=jax.ShapeDtypeStruct(arrived.shape[1:], F32), compiler_params=small, name="add_up"
     )(arrived.reshape(width, part.shape[1]))

time: 90.3 us -> 89.8 us (level)
  waiting for transfers between devices: 7.2 us -> 5.77 us
    ppermute x2, waiting for transfers between devices: 3.12 us -> 1.04 us  [swapped(): return lax.ppermute(array, CORE, [(0, 1), (1, 0)])]
    pallas_call x1 -> x3, Pallas kernels: 3.37 us -> 4.68 us  [the longest x1 2.63 us: run_second_pass(): pl.pallas_call(second_pass, in_specs=[VMEM] * 10, out_specs=[VMEM] * len(...]
  transfers between devices with their start and end apart: 3 -> 3, of which waited for: 3 -> 3; matrix products, arithmetic and copies ran while one was open for 0% -> 0% of each run, Pallas kernels for 8% -> 9%
where the time goes in v4:
time: 89.8 us; the launch traced here: 89.5 us
  blocking collectives  54.8 us (61%)
  Pallas kernels  18.4 us (20%)
  starting transfers between devices  9.82 us (11%)
  waiting for transfers between devices  5.77 us (6%)
    all_to_all x4, blocking collectives, exchanged(): return lax.all_to_all(array, axes, split_axis=0, concat_axis=0, tiled=True)  54.8 us
    ppermute x2, starting transfers between devices, swapped(): return lax.ppermute(array, CORE, [(0, 1), (1, 0)])  6.06 us
    all_to_all x1, waiting for transfers between devices, exchanged(): return lax.all_to_all(array, axes, split_axis=0, concat_axis=0, tiled=True)  4.73 us
    pallas_call x1, Pallas kernels, run_first_pass(): pl.pallas_call(first_pass, in_specs=[HBM] * 3, out_specs=[VMEM] * len(sha...  3.97 us
    pallas_call x1, Pallas kernels, run_token_outputs(): pl.pallas_call(token_outputs, grid=(clips, rows // block), in_specs=[pl.B...  3.77 us
    all_to_all x1, starting transfers between devices, exchanged(): return lax.all_to_all(array, axes, split_axis=0, concat_axis=0, tiled=True)  3.76 us
    pallas_call x1, Pallas kernels, run_second_pass(): pl.pallas_call(second_pass, in_specs=[VMEM] * 10, out_specs=[VMEM] * len(...  2.63 us
    pallas_call x1, Pallas kernels, run_weight_grads(): pl.pallas_call(weight_grads, grid=(count,), in_specs=[whole(total, width)...  2.55 us
  transfers between devices with their start and end apart: 3, of which 3 were waited for; matrix products, arithmetic and copies ran while one was open for 0% of the time, Pallas kernels for 9%

profile of v4, /device:TPU:1, one launch (start us, length us, event | category | flops | bytes accessed | tf_op | source)
XLA Modules:
  0.0 89.5 jit_solution(6641544476730708274)
XLA Ops:
  0.6 4.0 %first_pass.1 = (bf16[2,768,1024]{2,1,0:T(8,128)(2,1)S(1)}, bf16[1024,1536]{1,0:T(8,128)(2,1)S(1)}, bf16[2,768,1024]{2,1,0:T(8,128)(2,1)S(1)}, bf16[128,1024]{1,...) custom-call(bf16[2,768,1024]{2,1,0:T(8,128)(2,1)} %tok_hbm.1, ...), custom_call_target="tpu_custom_call" | custom-call | tf_op jit(solution)/shard_map/first_pass/pallas_call | solution.py:146
  4.6 1.5 %collective-permute-start = (bf16[8,8,4224]{2,1,0:T(8,128)(2,1)S(1)}, bf16[8,8,4224]{2,1,0:T(8,128)(2,1)S(1)}, u32[]{:S(2)}, u32[]{:S(2)}) collective-permute-start(bf16[8,8,4224]{2,1,0:T(8,128)(2,1)S(1)} %get-tuple-element.44), channel_id=1, source_target_pairs={{0,1},{1,0},{2,3},{3,2},{4,5},{5,4},{6,7},{7,6},{8,9},{9,8},{10,11... | collective-permute-start | bytes 1622024 | tf_op jit(solution)/shard_map/ppermute | solution.py:469
  6.1 0.9 turn.1.grad_t_ref
  7.0 0.0 copy-start
  7.0 0.0 copy-start.1
  7.0 0.7 collective-permute-done.recv_ref
  7.7 0.3 merge_cores.1
  8.0 19.4 %all_to_all.25.in_ref = bf16[8,8,4224]{2,1,0:T(8,128)(2,1)S(1)} all-to-all(bf16[8,8,4224]{2,1,0:T(8,128)(2,1)S(1)} %merge_cores.1), channel_id=1, replica_groups=mesh['seq_0'=2,'seq_1'=4,'exp_0'=2,'exp_1'=4,'exp_2'=2] {'exp_0','exp_1'}, dimensions={0} | all-to-all | bytes 1081344 | tf_op jit(solution)/shard_map/all_to_all | solution.py:465
  27.4 0.3 merge_column.1
  27.7 13.2 %all_to_all.26.in_ref = bf16[8,8,4224]{2,1,0:T(8,128)(2,1)S(1)} all-to-all(bf16[8,8,4224]{2,1,0:T(8,128)(2,1)S(1)} %merge_column.1), channel_id=1, replica_groups=mesh['seq_0'=2,'seq_1'=4,'exp_0'=2,'exp_1'=4,'exp_2'=2] {'seq_0','seq_1'}, dimensions={0} | all-to-all | bytes 1081344 | tf_op jit(solution)/shard_map/all_to_all | solution.py:465
  40.9 0.0 copy-done
  40.9 2.0 %experts.1 = (bf16[8,32,1024]{2,1,0:T(8,128)(2,1)S(1)}, bf16[16,1024]{1,0:T(8,128)(2,1)S(1)}, bf16[16,1024]{1,0:T(8,128)(2,1)S(1)}, bf16[16,512]{1,0:T(8,128)(2,...) custom-call(bf16[8,8,4224]{2,1,0:T(8,128)(2,1)S(1)} %all_to_all.26.in_ref, ...), custom_call_target="tpu_custom_call" | custom-call | tf_op jit(solution)/shard_map/experts/pallas_call | solution.py:250
  42.9 10.4 %all_to_all.27.in_ref = bf16[8,32,1024]{2,1,0:T(8,128)(2,1)S(1)} all-to-all(bf16[8,32,1024]{2,1,0:T(8,128)(2,1)S(1)} %get-tuple-element.52), channel_id=1, replica_groups=mesh['seq_0'=2,'seq_1'=4,'exp_0'=2,'exp_1'=4,'exp_2'=2] {'seq_0','seq_1'}, dimensions={0} | all-to-all | bytes 1048576 | tf_op jit(solution)/shard_map/all_to_all | solution.py:465
  53.3 0.1 slot_results.1
  53.4 11.8 %all_to_all.28.slots_ref = bf16[8,8,4224]{2,1,0:T(8,128)(2,1)S(1)} all-to-all(bf16[8,8,4224]{2,1,0:T(8,128)(2,1)S(1)} %slot_results.1), channel_id=1, replica_groups=mesh['seq_0'=2,'seq_1'=4,'exp_0'=2,'exp_1'=4,'exp_2'=2] {'exp_0','exp_1'}, dimensions={0} | all-to-all | bytes 1081344 | tf_op jit(solution)/shard_map/all_to_all | solution.py:465
  65.2 4.6 %collective-permute-start.1 = (bf16[8,8,4224]{2,1,0:T(8,128)(2,1)S(1)}, bf16[8,8,4224]{2,1,0:T(8,128)(2,1)S(1)}, u32[]{:S(2)}, u32[]{:S(2)}) collective-permute-start(bf16[8,8,4224]{2,1,0:T(8,128)(2,1)S(1)} %all_to_all.28.slots_ref), channel_id=1, source_target_pairs={{0,1},{1,0},{2,3},{3,2},{4,5},{5,4},{6,7},{7,6},{8,9},{9,8},{10,11... | collective-permute-start | bytes 1622024 | tf_op jit(solution)/shard_map/ppermute | solution.py:469
  69.8 1.2 %half_products.1 = (bf16[2,64,1024]{2,1,0:T(8,128)(2,1)S(1)}, bf16[2,64,1024]{2,1,0:T(8,128)(2,1)S(1)}, f32[64,128]{1,0:T(8,128)S(1)}, f32[2,64,768]{2,1,0:T(8,128)S(1)}, f32[2,64,768]{2,1,0:T(8,128)S(1)}) custom-call(bf16[1024,1536]{1,0:T(8,128)(2,1)S(1)} %get-tuple-element.43.tok_t_ref, bf16[1024,1536]{1,0:T(8,128)(2,1)S(1)} %turn.1.grad_t_ref, ...), custom_call_target="tpu_custom_call" | custom-call | tf_op jit(solution)/shard_map/half_products/pallas_call | solution.py:349
  71.0 0.4 collective-permute-done.1.slots_ref
  71.3 2.6 %second_pass.1 = (bf16[2,64,1024]{2,1,0:T(8,128)(2,1)S(1)}, bf16[2,64,1024]{2,1,0:T(8,128)(2,1)S(1)}, bf16[2,256,768]{2,1,0:T(8,128)(2,1)S(1)}, bf16[1024,128]{1,0:T(8,128)(2,1)}) custom-call(bf16[2,768,1024]{2,1,0:T(8,128)(2,1)S(1)} %get-tuple-element.42.tok_ref, bf16[1024,1536]{1,0:T(8,128)(2,1)S(1)} %get-tuple-element.43.tok_t_ref, ...), custom_call_target="tpu_custom_call" | custom-call | tf_op jit(solution)/shard_map/second_pass/pallas_call | solution.py:402
  74.0 3.8 %all-to-all-start.4 = ((bf16[128,8,128]{2,1,0:T(8,128)(2,1)}), bf16[128,8,128]{2,1,0:T(8,128)(2,1)S(1)}, u32[]{:S(2)}, u32[]{:S(2)}) async-start(bf16[128,8,128]{2,1,0:T(8,128)(2,1)} %bitcast), calls=%async_computation.4 | async-start | bytes 524288 | tf_op jit(solution)/shard_map/all_to_all | solution.py:465
  77.7 2.5 %weight_grads.1 = (bf16[2,1024,512]{2,1,0:T(8,128)(2,1)}, bf16[2,512,1024]{2,1,0:T(8,128)(2,1)}) custom-call(bf16[16,1024]{1,0:T(8,128)(2,1)S(1)} %get-tuple-element.71.rows_ref, bf16[16,1024]{1,0:T(8,128)(2,1)S(1)} %get-tuple-element.72.grads_ref, bf16[16,512]{1,0:T(8,128)(2,1)S(1)} %get-tuple-element.73.hidden_ref, ...), custom_call_target="tpu_custom_call" | custom-call | flops 67108864 | bytes 4194304 | tf_op jit(solution)/shard_map/weight_grads/pallas_call | solution.py:282
  80.3 3.8 %token_outputs.1 = (bf16[2,768,1024]{2,1,0:T(8,128)(2,1)}, bf16[2,768,1024]{2,1,0:T(8,128)(2,1)}) custom-call(bf16[2,128,768]{2,1,0:T(8,128)(2,1)S(1)} %get-tuple-element.41.mix_ref, bf16[2,256,768]{2,1,0:T(8,128)(2,1)S(1)} %get-tuple-element.62.weights_ref, bf16[2,64,1024]{2,1,0:T(8,128)(2,1)S(1)} %get-tuple-element.63.own_outs_ref, ...), custom_call_target="tpu_custom_call" | custom-call | flops 1207959552 | bytes 9437184 | tf_op jit(solution)/shard_map/token_outputs/pallas_call | solution.py:434
  84.0 4.7 %all-to-all-done.4 = bf16[128,8,128]{2,1,0:T(8,128)(2,1)S(1)} async-done(((bf16[128,8,128]{2,1,0:T(8,128)(2,1)}), bf16[128,8,128]{2,1,0:T(8,128)(2,1)S(1)}, u32[]{:S(2)}, u32[]{:S(2)}) %all-to-all-start.4) | async-done | bytes 262176 | tf_op jit(solution)/shard_map/all_to_all | solution.py:465
  88.8 0.7 add_up.1
  (1 shorter events, 0.0 us)
Async XLA Ops:
  4.6 3.1 %collective-permute-start = (bf16[8,8,4224]{2,1,0:T(8,128)(2,1)S(1)}, bf16[8,8,4224]{2,1,0:T(8,128)(2,1)S(1)}, u32[]{:S(2)}, u32[]{:S(2)}) collective-permute-start(bf16[8,8,4224]{2,1,0:T(8,128)(2,1)S(1)} %get-tuple-element.44), channel_id=1, source_target_pairs={{0,1},{1,0},{2,3},{3,2},{4,5},{5,4},{6,7},{7,6},{8,9},{9,8},{10,11... | collective-permute-start | bytes 1622024 | tf_op jit(solution)/shard_map/ppermute | solution.py:469
  7.0 33.9 %copy-start = (bf16[2,1024,512]{2,1,0:T(8,128)(2,1)S(1)}, bf16[2,1024,512]{2,1,0:T(8,128)(2,1)}, u32[]{:S(2)}) copy-start(bf16[2,1024,512]{2,1,0:T(8,128)(2,1)} %w_in_ref.1) | copy-start | bytes 6291460
  7.0 33.9 %copy-start.1 = (bf16[2,512,1024]{2,1,0:T(8,128)(2,1)S(1)}, bf16[2,512,1024]{2,1,0:T(8,128)(2,1)}, u32[]{:S(2)}) copy-start(bf16[2,512,1024]{2,1,0:T(8,128)(2,1)} %w_out_ref.1) | copy-start | bytes 6291460
  65.2 6.1 %collective-permute-start.1 = (bf16[8,8,4224]{2,1,0:T(8,128)(2,1)S(1)}, bf16[8,8,4224]{2,1,0:T(8,128)(2,1)S(1)}, u32[]{:S(2)}, u32[]{:S(2)}) collective-permute-start(bf16[8,8,4224]{2,1,0:T(8,128)(2,1)S(1)} %all_to_all.28.slots_ref), channel_id=1, source_target_pairs={{0,1},{1,0},{2,3},{3,2},{4,5},{5,4},{6,7},{7,6},{8,9},{9,8},{10,11... | collective-permute-start | bytes 1622024 | tf_op jit(solution)/shard_map/ppermute | solution.py:469
  74.0 14.8 %all-to-all-start.4 = ((bf16[128,8,128]{2,1,0:T(8,128)(2,1)}), bf16[128,8,128]{2,1,0:T(8,128)(2,1)S(1)}, u32[]{:S(2)}, u32[]{:S(2)}) async-start(bf16[128,8,128]{2,1,0:T(8,128)(2,1)} %bitcast), calls=%async_computation.4 | async-start | bytes 524288 | tf_op jit(solution)/shard_map/all_to_all | solution.py:465

commit v5 on v4

--- a/solution.py
+++ b/solution.py
@@ -84,19 +84,19 @@
         side = core if k < half // GROUP else 1 - core
         at = pl.ds(pl.multiple_of((2 * place + side) * GROUP, GROUP), GROUP)
         router_t_ref[pl.ds(k * GROUP, GROUP), :] = router_f[at, :].astype(BF16)
-    columns = [None] * 6
+    columns = [None] * 12
     for c in range(clips):
         copies[1 + c].wait()
         tok_t_ref[:, pl.ds(c * rows, rows)] = tok_ref[c].T
     both = dot_nn(router_t_ref[...], tok_t_ref[...])
     for c in range(clips):
         logits_t = both[:, c * rows : (c + 1) * rows]
-        peak = jnp.max(logits_t, axis=1, keepdims=True).astype(BF16).astype(F32)
+        peak = jnp.max(logits_t, axis=1, keepdims=True)
         terms = jnp.exp(logits_t - peak)
         terms_ref[c] = terms
         mass = jnp.sum(terms, axis=1, keepdims=True)
-        columns[c] = peak
-        columns[2 + 2 * c : 4 + 2 * c] = pieces(mass, 2)
+        columns[3 * c : 3 * c + 3] = pieces(peak, 3)
+        columns[6 + 3 * c : 9 + 3 * c] = pieces(mass, 3)
         sums = dot_nn(terms.astype(BF16), tok_ref[c]).astype(BF16)
         mixing = mixing_of(logits_t)
         mixing_ref[c] = mixing
@@ -158,17 +158,18 @@
     )(*(pltpu.with_memory_space_constraint(a, pltpu.HBM) for a in (tokens, router, grad_out)))
 
 
+def whole_of(tile, at):
+    return tile[:, at : at + 1] + tile[:, at + 1 : at + 2] + tile[:, at + 2 : at + 3]
+
+
 def merged(blocks, width):
     tiles = [load(4 * width, LANES) for load in blocks]
-    top = functools.reduce(jnp.maximum, tiles)
-    scales = [jnp.exp(jnp.minimum(tile - top, 0.0)) for tile in tiles]
     inputs, grads, peaks, masses = [], [], [], []
     for c in range(2):
-        peaks.append(top[:, c : c + 1])
-        columns = [scale[:, c : c + 1] for scale in scales]
-        masses.append(
-            sum(col * (t[:, 2 + 2 * c : 3 + 2 * c] + t[:, 3 + 2 * c : 4 + 2 * c]) for col, t in zip(columns, tiles))
-        )
+        tops = [whole_of(tile, 3 * c) for tile in tiles]
+        peaks.append(functools.reduce(jnp.maximum, tops))
+        columns = [jnp.exp(top - peaks[c]) for top in tops]
+        masses.append(sum(col * whole_of(tile, 6 + 3 * c) for col, tile in zip(columns, tiles)))
         inputs.append(sum(col * load(c * width, width) for col, load in zip(columns, blocks)))
         grads.append(sum(load((2 + c) * width, width) for load in blocks))
     return inputs, grads, peaks, masses
@@ -179,7 +180,7 @@
 
 
 def stat_tile(peaks, masses):
-    return packed([peaks[0], peaks[1], *pieces(masses[0], 2), *pieces(masses[1], 2)])
+    return packed([piece for value in (*peaks, *masses) for piece in pieces(value, 3)])
 
 
 def merge_cores(keep_ref, recv_ref, out_ref):
@@ -213,7 +214,7 @@
     inputs, grads, peaks, masses = merged(blocks, width)
     slot_in = jnp.concatenate([value / mass for value, mass in zip(inputs, masses)], axis=0)
     slot_in_ref[...] = slot_in
-    stats_ref[...] = packed([*peaks, *pieces(masses[0], 3), *pieces(masses[1], 3)])
+    stats_ref[...] = stat_tile(peaks, masses)
     x = slot_in.astype(BF16)
     g = jnp.concatenate(grads, axis=0).astype(BF16)
     rows_ref[...] = x
@@ -308,7 +309,7 @@
     lane = lax.broadcasted_iota(jnp.int32, tile.shape, 1)
     for c in range(2):
         for k, column in enumerate(pieces(inner[c * GROUP : (c + 1) * GROUP], 3)):
-            tile = jnp.where(lane == 8 + 3 * c + k, column, tile)
+            tile = jnp.where(lane == 12 + 3 * c + k, column, tile)
     for q in range(out_ref.shape[0]):
         for k in range(4):
             out_ref[q, :, pl.ds(k * width, width)] = total[k * GROUP : (k + 1) * GROUP]
@@ -370,12 +371,10 @@
     )
     tile = jnp.concatenate([own_stats_ref[...], stats_ref[...]], axis=0)
     local = local_ref[...]
-    column = lambda k: tile[:, k : k + 1]
     total = jnp.zeros((slots, width), F32)
     for c in range(clips):
-        mass = column(2 + 3 * c) + column(3 + 3 * c) + column(4 + 3 * c)
-        inner = column(8 + 3 * c) + column(9 + 3 * c) + column(10 + 3 * c)
-        scale = jnp.exp(local[:, c : c + 1] - column(c)) / mass
+        mass, inner = whole_of(tile, 6 + 3 * c), whole_of(tile, 12 + 3 * c)
+        scale = jnp.exp(whole_of(local, 3 * c) - whole_of(tile, 3 * c)) / mass
         dispatch = terms_ref[c] * scale
         weights_ref[c, pl.ds(0, slots), :] = dispatch.astype(BF16)
         mixing = mixing_ref[c]

time: 89.8 us -> 89.9 us (level)
  no operation moved by 1% of the time
where the time goes in v5:
time: 89.9 us; the launch traced here: 89.6 us
  blocking collectives  54.8 us (61%)
  Pallas kernels  18.5 us (21%)
  starting transfers between devices  9.81 us (11%)
  waiting for transfers between devices  5.76 us (6%)
    all_to_all x4, blocking collectives, exchanged(): return lax.all_to_all(array, axes, split_axis=0, concat_axis=0, tiled=True)  54.8 us
    ppermute x2, starting transfers between devices, swapped(): return lax.ppermute(array, CORE, [(0, 1), (1, 0)])  6.05 us
    all_to_all x1, waiting for transfers between devices, exchanged(): return lax.all_to_all(array, axes, split_axis=0, concat_axis=0, tiled=True)  4.73 us
    pallas_call x1, Pallas kernels, run_first_pass(): pl.pallas_call(first_pass, in_specs=[HBM] * 3, out_specs=[VMEM] * len(sha...  4.05 us
    pallas_call x1, Pallas kernels, run_token_outputs(): pl.pallas_call(token_outputs, grid=(clips, rows // block), in_specs=[pl.B...  3.77 us
    all_to_all x1, starting transfers between devices, exchanged(): return lax.all_to_all(array, axes, split_axis=0, concat_axis=0, tiled=True)  3.76 us
    pallas_call x1, Pallas kernels, run_second_pass(): pl.pallas_call(second_pass, in_specs=[VMEM] * 10, out_specs=[VMEM] * len(...  2.61 us
    pallas_call x1, Pallas kernels, run_weight_grads(): pl.pallas_call(weight_grads, grid=(count,), in_specs=[whole(total, width)...  2.55 us
  transfers between devices with their start and end apart: 3, of which 3 were waited for; matrix products, arithmetic and copies ran while one was open for 0% of the time, Pallas kernels for 9%

profile of v5, /device:TPU:1, one launch (start us, length us, event | category | flops | bytes accessed | tf_op | source)
XLA Modules:
  0.0 89.6 jit_solution(13881567749313579690)
XLA Ops:
  0.6 4.1 %first_pass.1 = (bf16[2,768,1024]{2,1,0:T(8,128)(2,1)S(1)}, bf16[1024,1536]{1,0:T(8,128)(2,1)S(1)}, bf16[2,768,1024]{2,1,0:T(8,128)(2,1)S(1)}, bf16[128,1024]{1,...) custom-call(bf16[2,768,1024]{2,1,0:T(8,128)(2,1)} %tok_hbm.1, ...), custom_call_target="tpu_custom_call" | custom-call | tf_op jit(solution)/shard_map/first_pass/pallas_call | solution.py:146
  4.7 1.5 %collective-permute-start = (bf16[8,8,4224]{2,1,0:T(8,128)(2,1)S(1)}, bf16[8,8,4224]{2,1,0:T(8,128)(2,1)S(1)}, u32[]{:S(2)}, u32[]{:S(2)}) collective-permute-start(bf16[8,8,4224]{2,1,0:T(8,128)(2,1)S(1)} %get-tuple-element.44), channel_id=1, source_target_pairs={{0,1},{1,0},{2,3},{3,2},{4,5},{5,4},{6,7},{7,6},{8,9},{9,8},{10,11... | collective-permute-start | bytes 1622024 | tf_op jit(solution)/shard_map/ppermute | solution.py:468
  6.2 0.9 turn.1.grad_t_ref
  7.1 0.0 copy-start
  7.1 0.0 copy-start.1
  7.1 0.7 collective-permute-done.recv_ref
  7.8 0.3 merge_cores.1
  8.1 19.4 %all_to_all.25.in_ref = bf16[8,8,4224]{2,1,0:T(8,128)(2,1)S(1)} all-to-all(bf16[8,8,4224]{2,1,0:T(8,128)(2,1)S(1)} %merge_cores.1), channel_id=1, replica_groups=mesh['seq_0'=2,'seq_1'=4,'exp_0'=2,'exp_1'=4,'exp_2'=2] {'exp_0','exp_1'}, dimensions={0} | all-to-all | bytes 1081344 | tf_op jit(solution)/shard_map/all_to_all | solution.py:464
  27.5 0.3 merge_column.1
  27.8 13.2 %all_to_all.26.in_ref = bf16[8,8,4224]{2,1,0:T(8,128)(2,1)S(1)} all-to-all(bf16[8,8,4224]{2,1,0:T(8,128)(2,1)S(1)} %merge_column.1), channel_id=1, replica_groups=mesh['seq_0'=2,'seq_1'=4,'exp_0'=2,'exp_1'=4,'exp_2'=2] {'seq_0','seq_1'}, dimensions={0} | all-to-all | bytes 1081344 | tf_op jit(solution)/shard_map/all_to_all | solution.py:464
  41.0 0.0 copy-done
  41.0 2.0 %experts.1 = (bf16[8,32,1024]{2,1,0:T(8,128)(2,1)S(1)}, bf16[16,1024]{1,0:T(8,128)(2,1)S(1)}, bf16[16,1024]{1,0:T(8,128)(2,1)S(1)}, bf16[16,512]{1,0:T(8,128)(2,...) custom-call(bf16[8,8,4224]{2,1,0:T(8,128)(2,1)S(1)} %all_to_all.26.in_ref, ...), custom_call_target="tpu_custom_call" | custom-call | tf_op jit(solution)/shard_map/experts/pallas_call | solution.py:251
  43.0 10.4 %all_to_all.27.in_ref = bf16[8,32,1024]{2,1,0:T(8,128)(2,1)S(1)} all-to-all(bf16[8,32,1024]{2,1,0:T(8,128)(2,1)S(1)} %get-tuple-element.52), channel_id=1, replica_groups=mesh['seq_0'=2,'seq_1'=4,'exp_0'=2,'exp_1'=4,'exp_2'=2] {'seq_0','seq_1'}, dimensions={0} | all-to-all | bytes 1048576 | tf_op jit(solution)/shard_map/all_to_all | solution.py:464
  53.4 0.1 slot_results.1
  53.5 11.8 %all_to_all.28.slots_ref = bf16[8,8,4224]{2,1,0:T(8,128)(2,1)S(1)} all-to-all(bf16[8,8,4224]{2,1,0:T(8,128)(2,1)S(1)} %slot_results.1), channel_id=1, replica_groups=mesh['seq_0'=2,'seq_1'=4,'exp_0'=2,'exp_1'=4,'exp_2'=2] {'exp_0','exp_1'}, dimensions={0} | all-to-all | bytes 1081344 | tf_op jit(solution)/shard_map/all_to_all | solution.py:464
  65.3 4.6 %collective-permute-start.1 = (bf16[8,8,4224]{2,1,0:T(8,128)(2,1)S(1)}, bf16[8,8,4224]{2,1,0:T(8,128)(2,1)S(1)}, u32[]{:S(2)}, u32[]{:S(2)}) collective-permute-start(bf16[8,8,4224]{2,1,0:T(8,128)(2,1)S(1)} %all_to_all.28.slots_ref), channel_id=1, source_target_pairs={{0,1},{1,0},{2,3},{3,2},{4,5},{5,4},{6,7},{7,6},{8,9},{9,8},{10,11... | collective-permute-start | bytes 1622024 | tf_op jit(solution)/shard_map/ppermute | solution.py:468
  69.9 1.2 %half_products.1 = (bf16[2,64,1024]{2,1,0:T(8,128)(2,1)S(1)}, bf16[2,64,1024]{2,1,0:T(8,128)(2,1)S(1)}, f32[64,128]{1,0:T(8,128)S(1)}, f32[2,64,768]{2,1,0:T(8,128)S(1)}, f32[2,64,768]{2,1,0:T(8,128)S(1)}) custom-call(bf16[1024,1536]{1,0:T(8,128)(2,1)S(1)} %get-tuple-element.43.tok_t_ref, bf16[1024,1536]{1,0:T(8,128)(2,1)S(1)} %turn.1.grad_t_ref, ...), custom_call_target="tpu_custom_call" | custom-call | tf_op jit(solution)/shard_map/half_products/pallas_call | solution.py:350
  71.1 0.4 collective-permute-done.1.slots_ref
  71.4 2.6 %second_pass.1 = (bf16[2,64,1024]{2,1,0:T(8,128)(2,1)S(1)}, bf16[2,64,1024]{2,1,0:T(8,128)(2,1)S(1)}, bf16[2,256,768]{2,1,0:T(8,128)(2,1)S(1)}, bf16[1024,128]{1,0:T(8,128)(2,1)}) custom-call(bf16[2,768,1024]{2,1,0:T(8,128)(2,1)S(1)} %get-tuple-element.42.tok_ref, bf16[1024,1536]{1,0:T(8,128)(2,1)S(1)} %get-tuple-element.43.tok_t_ref, ...), custom_call_target="tpu_custom_call" | custom-call | tf_op jit(solution)/shard_map/second_pass/pallas_call | solution.py:401
  74.1 3.8 %all-to-all-start.4 = ((bf16[128,8,128]{2,1,0:T(8,128)(2,1)}), bf16[128,8,128]{2,1,0:T(8,128)(2,1)S(1)}, u32[]{:S(2)}, u32[]{:S(2)}) async-start(bf16[128,8,128]{2,1,0:T(8,128)(2,1)} %bitcast), calls=%async_computation.4 | async-start | bytes 524288 | tf_op jit(solution)/shard_map/all_to_all | solution.py:464
  77.8 2.6 %weight_grads.1 = (bf16[2,1024,512]{2,1,0:T(8,128)(2,1)}, bf16[2,512,1024]{2,1,0:T(8,128)(2,1)}) custom-call(bf16[16,1024]{1,0:T(8,128)(2,1)S(1)} %get-tuple-element.71.rows_ref, bf16[16,1024]{1,0:T(8,128)(2,1)S(1)} %get-tuple-element.72.grads_ref, bf16[16,512]{1,0:T(8,128)(2,1)S(1)} %get-tuple-element.73.hidden_ref, ...), custom_call_target="tpu_custom_call" | custom-call | flops 67108864 | bytes 4194304 | tf_op jit(solution)/shard_map/weight_grads/pallas_call | solution.py:283
  80.4 3.8 %token_outputs.1 = (bf16[2,768,1024]{2,1,0:T(8,128)(2,1)}, bf16[2,768,1024]{2,1,0:T(8,128)(2,1)}) custom-call(bf16[2,128,768]{2,1,0:T(8,128)(2,1)S(1)} %get-tuple-element.41.mix_ref, bf16[2,256,768]{2,1,0:T(8,128)(2,1)S(1)} %get-tuple-element.62.weights_ref, bf16[2,64,1024]{2,1,0:T(8,128)(2,1)S(1)} %get-tuple-element.63.own_outs_ref, ...), custom_call_target="tpu_custom_call" | custom-call | flops 1207959552 | bytes 9437184 | tf_op jit(solution)/shard_map/token_outputs/pallas_call | solution.py:433
  84.1 4.7 %all-to-all-done.4 = bf16[128,8,128]{2,1,0:T(8,128)(2,1)S(1)} async-done(((bf16[128,8,128]{2,1,0:T(8,128)(2,1)}), bf16[128,8,128]{2,1,0:T(8,128)(2,1)S(1)}, u32[]{:S(2)}, u32[]{:S(2)}) %all-to-all-start.4) | async-done | bytes 262176 | tf_op jit(solution)/shard_map/all_to_all | solution.py:464
  88.9 0.7 add_up.1
  (1 shorter events, 0.0 us)
Async XLA Ops:
  4.7 3.1 %collective-permute-start = (bf16[8,8,4224]{2,1,0:T(8,128)(2,1)S(1)}, bf16[8,8,4224]{2,1,0:T(8,128)(2,1)S(1)}, u32[]{:S(2)}, u32[]{:S(2)}) collective-permute-start(bf16[8,8,4224]{2,1,0:T(8,128)(2,1)S(1)} %get-tuple-element.44), channel_id=1, source_target_pairs={{0,1},{1,0},{2,3},{3,2},{4,5},{5,4},{6,7},{7,6},{8,9},{9,8},{10,11... | collective-permute-start | bytes 1622024 | tf_op jit(solution)/shard_map/ppermute | solution.py:468
  7.1 33.9 %copy-start = (bf16[2,1024,512]{2,1,0:T(8,128)(2,1)S(1)}, bf16[2,1024,512]{2,1,0:T(8,128)(2,1)}, u32[]{:S(2)}) copy-start(bf16[2,1024,512]{2,1,0:T(8,128)(2,1)} %w_in_ref.1) | copy-start | bytes 6291460
  7.1 33.9 %copy-start.1 = (bf16[2,512,1024]{2,1,0:T(8,128)(2,1)S(1)}, bf16[2,512,1024]{2,1,0:T(8,128)(2,1)}, u32[]{:S(2)}) copy-start(bf16[2,512,1024]{2,1,0:T(8,128)(2,1)} %w_out_ref.1) | copy-start | bytes 6291460
  65.3 6.1 %collective-permute-start.1 = (bf16[8,8,4224]{2,1,0:T(8,128)(2,1)S(1)}, bf16[8,8,4224]{2,1,0:T(8,128)(2,1)S(1)}, u32[]{:S(2)}, u32[]{:S(2)}) collective-permute-start(bf16[8,8,4224]{2,1,0:T(8,128)(2,1)S(1)} %all_to_all.28.slots_ref), channel_id=1, source_target_pairs={{0,1},{1,0},{2,3},{3,2},{4,5},{5,4},{6,7},{7,6},{8,9},{9,8},{10,11... | collective-permute-start | bytes 1622024 | tf_op jit(solution)/shard_map/ppermute | solution.py:468
  74.1 14.8 %all-to-all-start.4 = ((bf16[128,8,128]{2,1,0:T(8,128)(2,1)}), bf16[128,8,128]{2,1,0:T(8,128)(2,1)S(1)}, u32[]{:S(2)}, u32[]{:S(2)}) async-start(bf16[128,8,128]{2,1,0:T(8,128)(2,1)} %bitcast), calls=%async_computation.4 | async-start | bytes 524288 | tf_op jit(solution)/shard_map/all_to_all | solution.py:464

commit v6 on v5

--- a/solution.py
+++ b/solution.py
@@ -62,8 +62,8 @@
 
 
 def first_pass(
-    tok_hbm, router_hbm, grad_hbm,
-    tok_ref, tok_t_ref, grad_ref, router_t_ref, terms_ref, mixing_ref, mix_ref, stats_ref, keep_ref, send_ref,
+    tok_hbm, router_hbm, grad_hbm, w_out_hbm,
+    tok_ref, tok_t_ref, grad_ref, router_t_ref, terms_ref, mixing_ref, mix_ref, stats_ref, keep_ref, send_ref, w_out_ref,
     router_buf, router_f, sems,
 ):
     core = lax.axis_index(CORE)
@@ -75,6 +75,7 @@
         copies.append(pltpu.make_async_copy(tok_hbm.at[c], tok_ref.at[c], sems.at[1 + c]))
     for c in range(clips):
         copies.append(pltpu.make_async_copy(grad_hbm.at[c], grad_ref.at[c], sems.at[1 + clips + c]))
+    copies.append(pltpu.make_async_copy(w_out_hbm, w_out_ref, sems.at[1 + 2 * clips]))
     for copy in copies:
         copy.start()
     copies[0].wait()
@@ -120,13 +121,14 @@
             at = pl.ds((2 + c) * width, width)
             keep_ref[q, :, at] = sums[q * GROUP : (q + 1) * GROUP]
             send_ref[q, :, at] = sums[half + q * GROUP : half + (q + 1) * GROUP]
+    copies[1 + 2 * clips].wait()
 
 
 VMEM = pl.BlockSpec(memory_space=pltpu.VMEM)
 HBM = pl.BlockSpec(memory_space=pltpu.HBM)
 
 
-def run_first_pass(tokens, router, grad_out):
+def run_first_pass(tokens, router, grad_out, w_out):
     clips, rows, width = tokens.shape
     slots = router.shape[1]
     row = 4 * width + LANES
@@ -142,20 +144,21 @@
         ((slots, LANES), F32),
         ((groups, GROUP, row), BF16),
         ((groups, GROUP, row), BF16),
+        (w_out.shape, BF16),
     ]
     return pl.pallas_call(
         first_pass,
-        in_specs=[HBM] * 3,
+        in_specs=[HBM] * 4,
         out_specs=[VMEM] * len(shapes),
         out_shape=[jax.ShapeDtypeStruct(*shape) for shape in shapes],
         scratch_shapes=[
             pltpu.VMEM(router.shape, BF16),
             pltpu.VMEM((slots, width), F32),
-            pltpu.SemaphoreType.DMA((1 + 2 * clips,)),
+            pltpu.SemaphoreType.DMA((2 + 2 * clips,)),
         ],
         compiler_params=params(28),
         name="first_pass",
-    )(*(pltpu.with_memory_space_constraint(a, pltpu.HBM) for a in (tokens, router, grad_out)))
+    )(*(pltpu.with_memory_space_constraint(a, pltpu.HBM) for a in (tokens, router, grad_out, w_out)))
 
 
 def whole_of(tile, at):
@@ -207,7 +210,10 @@
 GELU_B = 0.044715
 
 
-def experts(in_ref, w_in_ref, w_out_ref, out_ref, rows_ref, grads_ref, hidden_ref, pre_grad_ref, slot_in_ref, stats_ref):
+def experts(
+    in_ref, w_in_ref, w_out_ref, w_out_t_ref,
+    out_ref, rows_ref, grads_ref, hidden_ref, pre_grad_ref, slot_in_ref, stats_ref,
+):
     width = w_in_ref.shape[1]
     count = w_in_ref.shape[0]
     blocks = [loader(in_ref, k) for k in range(in_ref.shape[0])]
@@ -227,7 +233,7 @@
     hidden_grad = jnp.zeros((total, hid), F32)
     for e in range(count):
         pre = jnp.where(who == e, dot_nn(x, w_in_ref[e]), pre)
-        hidden_grad = jnp.where(who == e, dot_nt(g, w_out_ref[e]), hidden_grad)
+        hidden_grad = jnp.where(who == e, dot_nn(g, w_out_t_ref[e]), hidden_grad)
     inner = jnp.tanh(GELU_A * (pre + GELU_B * pre * pre * pre))
     hidden = 0.5 * pre * (1.0 + inner)
     slope = 0.5 * (1.0 + inner) + 0.5 * pre * (1.0 - inner * inner) * GELU_A * (1.0 + 3.0 * GELU_B * pre * pre)
@@ -244,7 +250,7 @@
         out_ref[q] = both
 
 
-def run_experts(sums, w_in, w_out):
+def run_experts(sums, w_in, w_out, w_out_t):
     count, width, hid = w_in.shape
     peers = sums.shape[0]
     rows = 2 * GROUP
@@ -261,7 +267,7 @@
         ],
         compiler_params=params(16),
         name="experts",
-    )(sums, w_in, w_out)
+    )(sums, w_in, w_out, w_out_t)
 
 
 def weight_grads(rows_ref, grads_ref, hidden_ref, pre_grad_ref, w_in_grad_ref, w_out_grad_ref):
@@ -316,10 +322,25 @@
         out_ref[q, :, pl.ds(4 * width, LANES)] = tile.astype(BF16)
 
 
-def turn(in_ref, out_ref):
-    rows = in_ref.shape[1]
-    for c in range(in_ref.shape[0]):
-        out_ref[:, pl.ds(c * rows, rows)] = in_ref[c].T
+def turn(grad_ref, w_out_ref, grad_t_ref, w_out_t_ref):
+    rows = grad_ref.shape[1]
+    for c in range(grad_ref.shape[0]):
+        grad_t_ref[:, pl.ds(c * rows, rows)] = grad_ref[c].T
+    for e in range(w_out_ref.shape[0]):
+        w_out_t_ref[e] = w_out_ref[e].T
+
+
+def run_turn(grad, w_out):
+    clips, rows, width = grad.shape
+    shapes = [(width, clips * rows), (w_out.shape[0], width, w_out.shape[1])]
+    return pl.pallas_call(
+        turn,
+        in_specs=[VMEM] * 2,
+        out_specs=[VMEM] * len(shapes),
+        out_shape=[jax.ShapeDtypeStruct(shape, BF16) for shape in shapes],
+        compiler_params=params(16),
+        name="turn",
+    )(grad, w_out)
 
 
 def half_products(tok_t_ref, grad_t_ref, slots_ref, outs_ref, backs_ref, stats_ref, dispatch_grad_ref, mixing_grad_ref):
@@ -473,25 +494,22 @@
     width = tokens.shape[2]
     row = 4 * width + LANES
     chips = lax.axis_size(CHIPS_EXP)
-    tok, tok_t, grad, router_t, terms, mixing, mix, local, keep, send = run_first_pass(tokens, router, grad_out)
+    tok, tok_t, grad, router_t, terms, mixing, mix, local, keep, send, w_out = run_first_pass(
+        tokens, router, grad_out, w_out
+    )
     recv = swapped(send)
     small = params(16)
-    grad_t = pl.pallas_call(
-        turn,
-        in_specs=[VMEM],
-        out_specs=VMEM,
-        out_shape=jax.ShapeDtypeStruct(tok_t.shape, BF16),
-        compiler_params=small,
-        name="turn",
-    )(grad)
-    recv, grad_t = lax.optimization_barrier((recv, grad_t))
+    grad_t, w_out_t = run_turn(grad, w_out)
+    recv, grad_t, w_out_t = lax.optimization_barrier((recv, grad_t, w_out_t))
     halves = pl.pallas_call(
         merge_cores, out_shape=jax.ShapeDtypeStruct((chips, GROUP, row), BF16), compiler_params=small, name="merge_cores"
     )(keep, recv)
     column = pl.pallas_call(
         merge_column, out_shape=jax.ShapeDtypeStruct((peers, GROUP, row), BF16), compiler_params=small, name="merge_column"
     )(exchanged(halves, CHIPS_EXP))
-    parts, rows, grads, hidden, pre_grad, slot_in, stats = run_experts(exchanged(column, SEQ), w_in, w_out)
+    parts, rows, grads, hidden, pre_grad, slot_in, stats = run_experts(
+        exchanged(column, SEQ), w_in, w_out, w_out_t
+    )
     arrived = exchanged(parts, SEQ)
     grad_w_in, grad_w_out = run_weight_grads(rows, grads, hidden, pre_grad, w_in.shape[0])
     results = pl.pallas_call(

time: 89.9 us -> 89.7 us (level)
  transfers between devices with their start and end apart: 3 -> 3, of which waited for: 3 -> 3; matrix products, arithmetic and copies ran while one was open for 0% -> 0% of each run, Pallas kernels for 9% -> 10%
where the time goes in v6:
time: 89.7 us; the launch traced here: 89.4 us
  blocking collectives  54.8 us (61%)
  Pallas kernels  18.8 us (21%)
  starting transfers between devices  9.83 us (11%)
  waiting for transfers between devices  5.24 us (6%)
    all_to_all x4, blocking collectives, exchanged(): return lax.all_to_all(array, axes, split_axis=0, concat_axis=0, tiled=True)  54.8 us
    ppermute x2, starting transfers between devices, swapped(): return lax.ppermute(array, CORE, [(0, 1), (1, 0)])  6.06 us
    all_to_all x1, waiting for transfers between devices, exchanged(): return lax.all_to_all(array, axes, split_axis=0, concat_axis=0, tiled=True)  4.73 us
    pallas_call x1, Pallas kernels, run_first_pass(): pl.pallas_call(first_pass, in_specs=[HBM] * 4, out_specs=[VMEM] * len(sha...  4.06 us
    pallas_call x1, Pallas kernels, run_token_outputs(): pl.pallas_call(token_outputs, grid=(clips, rows // block), in_specs=[pl.B...  3.77 us
    all_to_all x1, starting transfers between devices, exchanged(): return lax.all_to_all(array, axes, split_axis=0, concat_axis=0, tiled=True)  3.77 us
    pallas_call x1, Pallas kernels, run_second_pass(): pl.pallas_call(second_pass, in_specs=[VMEM] * 10, out_specs=[VMEM] * len(...  2.61 us
    pallas_call x1, Pallas kernels, run_weight_grads(): pl.pallas_call(weight_grads, grid=(count,), in_specs=[whole(total, width)...  2.55 us
  transfers between devices with their start and end apart: 3, of which 3 were waited for; matrix products, arithmetic and copies ran while one was open for 0% of the time, Pallas kernels for 10%

profile of v6, /device:TPU:1, one launch (start us, length us, event | category | flops | bytes accessed | tf_op | source)
XLA Modules:
  0.0 89.4 jit_solution(12941271652645192755)
XLA Ops:
  0.6 4.1 %first_pass.1 = (bf16[2,768,1024]{2,1,0:T(8,128)(2,1)S(1)}, bf16[1024,1536]{1,0:T(8,128)(2,1)S(1)}, bf16[2,768,1024]{2,1,0:T(8,128)(2,1)S(1)}, bf16[128,1024]{1,...) custom-call(bf16[2,768,1024]{2,1,0:T(8,128)(2,1)} %tok_hbm.1, ...), custom_call_target="tpu_custom_call" | custom-call | tf_op jit(solution)/shard_map/first_pass/pallas_call | solution.py:149
  4.7 1.5 %collective-permute-start = (bf16[8,8,4224]{2,1,0:T(8,128)(2,1)S(1)}, bf16[8,8,4224]{2,1,0:T(8,128)(2,1)S(1)}, u32[]{:S(2)}, u32[]{:S(2)}) collective-permute-start(bf16[8,8,4224]{2,1,0:T(8,128)(2,1)S(1)} %get-tuple-element.48), channel_id=1, source_target_pairs={{0,1},{1,0},{2,3},{3,2},{4,5},{5,4},{6,7},{7,6},{8,9},{9,8},{10,11... | collective-permute-start | bytes 1622024 | tf_op jit(solution)/shard_map/ppermute | solution.py:489
  6.2 1.4 %turn.1 = (bf16[1024,1536]{1,0:T(8,128)(2,1)S(1)}, bf16[2,1024,512]{2,1,0:T(8,128)(2,1)S(1)}) custom-call(bf16[2,768,1024]{2,1,0:T(8,128)(2,1)S(1)} %get-tuple-element.49.grad_ref, bf16[2,512,1024]{2,1,0:T(8,128)(2,1)S(1)} %get-tuple-element.50.w_out_ref), custom_call_target="tpu_custom_call" | custom-call | tf_op jit(solution)/shard_map/turn/pallas_call | solution.py:336
  7.6 0.0 copy-start
  7.6 0.1 collective-permute-done.recv_ref
  7.8 0.3 merge_cores.1
  8.1 19.4 %all_to_all.25.in_ref = bf16[8,8,4224]{2,1,0:T(8,128)(2,1)S(1)} all-to-all(bf16[8,8,4224]{2,1,0:T(8,128)(2,1)S(1)} %merge_cores.1), channel_id=1, replica_groups=mesh['seq_0'=2,'seq_1'=4,'exp_0'=2,'exp_1'=4,'exp_2'=2] {'exp_0','exp_1'}, dimensions={0} | all-to-all | bytes 1081344 | tf_op jit(solution)/shard_map/all_to_all | solution.py:485
  27.5 0.3 merge_column.1
  27.8 13.2 %all_to_all.26.in_ref = bf16[8,8,4224]{2,1,0:T(8,128)(2,1)S(1)} all-to-all(bf16[8,8,4224]{2,1,0:T(8,128)(2,1)S(1)} %merge_column.1), channel_id=1, replica_groups=mesh['seq_0'=2,'seq_1'=4,'exp_0'=2,'exp_1'=4,'exp_2'=2] {'seq_0','seq_1'}, dimensions={0} | all-to-all | bytes 1081344 | tf_op jit(solution)/shard_map/all_to_all | solution.py:485
  41.0 0.0 copy-done
  41.0 1.7 %experts.1 = (bf16[8,32,1024]{2,1,0:T(8,128)(2,1)S(1)}, bf16[16,1024]{1,0:T(8,128)(2,1)S(1)}, bf16[16,1024]{1,0:T(8,128)(2,1)S(1)}, bf16[16,512]{1,0:T(8,128)(2,...) custom-call(bf16[8,8,4224]{2,1,0:T(8,128)(2,1)S(1)} %all_to_all.26.in_ref, ...), custom_call_target="tpu_custom_call" | custom-call | tf_op jit(solution)/shard_map/experts/pallas_call | solution.py:257
  42.7 10.4 %all_to_all.27.in_ref = bf16[8,32,1024]{2,1,0:T(8,128)(2,1)S(1)} all-to-all(bf16[8,32,1024]{2,1,0:T(8,128)(2,1)S(1)} %get-tuple-element.60), channel_id=1, replica_groups=mesh['seq_0'=2,'seq_1'=4,'exp_0'=2,'exp_1'=4,'exp_2'=2] {'seq_0','seq_1'}, dimensions={0} | all-to-all | bytes 1048576 | tf_op jit(solution)/shard_map/all_to_all | solution.py:485
  53.1 0.1 slot_results.1
  53.2 11.8 %all_to_all.28.slots_ref = bf16[8,8,4224]{2,1,0:T(8,128)(2,1)S(1)} all-to-all(bf16[8,8,4224]{2,1,0:T(8,128)(2,1)S(1)} %slot_results.1), channel_id=1, replica_groups=mesh['seq_0'=2,'seq_1'=4,'exp_0'=2,'exp_1'=4,'exp_2'=2] {'exp_0','exp_1'}, dimensions={0} | all-to-all | bytes 1081344 | tf_op jit(solution)/shard_map/all_to_all | solution.py:485
  65.1 4.6 %collective-permute-start.1 = (bf16[8,8,4224]{2,1,0:T(8,128)(2,1)S(1)}, bf16[8,8,4224]{2,1,0:T(8,128)(2,1)S(1)}, u32[]{:S(2)}, u32[]{:S(2)}) collective-permute-start(bf16[8,8,4224]{2,1,0:T(8,128)(2,1)S(1)} %all_to_all.28.slots_ref), channel_id=1, source_target_pairs={{0,1},{1,0},{2,3},{3,2},{4,5},{5,4},{6,7},{7,6},{8,9},{9,8},{10,11... | collective-permute-start | bytes 1622024 | tf_op jit(solution)/shard_map/ppermute | solution.py:489
  69.6 1.2 %half_products.1 = (bf16[2,64,1024]{2,1,0:T(8,128)(2,1)S(1)}, bf16[2,64,1024]{2,1,0:T(8,128)(2,1)S(1)}, f32[64,128]{1,0:T(8,128)S(1)}, f32[2,64,768]{2,1,0:T(8,128)S(1)}, f32[2,64,768]{2,1,0:T(8,128)S(1)}) custom-call(bf16[1024,1536]{1,0:T(8,128)(2,1)S(1)} %get-tuple-element.47.tok_t_ref, bf16[1024,1536]{1,0:T(8,128)(2,1)S(1)} %get-tuple-element.53.grad_t_ref, ...), custom_call_target="tpu_custom_call" | custom-call | tf_op jit(solution)/shard_map/half_products/pallas_call | solution.py:371
  70.8 0.4 collective-permute-done.1.slots_ref
  71.2 2.6 %second_pass.1 = (bf16[2,64,1024]{2,1,0:T(8,128)(2,1)S(1)}, bf16[2,64,1024]{2,1,0:T(8,128)(2,1)S(1)}, bf16[2,256,768]{2,1,0:T(8,128)(2,1)S(1)}, bf16[1024,128]{1,0:T(8,128)(2,1)}) custom-call(bf16[2,768,1024]{2,1,0:T(8,128)(2,1)S(1)} %get-tuple-element.46.tok_ref, bf16[1024,1536]{1,0:T(8,128)(2,1)S(1)} %get-tuple-element.47.tok_t_ref, ...), custom_call_target="tpu_custom_call" | custom-call | tf_op jit(solution)/shard_map/second_pass/pallas_call | solution.py:422
  73.8 3.8 %all-to-all-start.4 = ((bf16[128,8,128]{2,1,0:T(8,128)(2,1)}), bf16[128,8,128]{2,1,0:T(8,128)(2,1)S(1)}, u32[]{:S(2)}, u32[]{:S(2)}) async-start(bf16[128,8,128]{2,1,0:T(8,128)(2,1)} %bitcast), calls=%async_computation.4 | async-start | bytes 524288 | tf_op jit(solution)/shard_map/all_to_all | solution.py:485
  77.6 2.6 %weight_grads.1 = (bf16[2,1024,512]{2,1,0:T(8,128)(2,1)}, bf16[2,512,1024]{2,1,0:T(8,128)(2,1)}) custom-call(bf16[16,1024]{1,0:T(8,128)(2,1)S(1)} %get-tuple-element.79.rows_ref, bf16[16,1024]{1,0:T(8,128)(2,1)S(1)} %get-tuple-element.80.grads_ref, bf16[16,512]{1,0:T(8,128)(2,1)S(1)} %get-tuple-element.81.hidden_ref, ...), custom_call_target="tpu_custom_call" | custom-call | flops 67108864 | bytes 4194304 | tf_op jit(solution)/shard_map/weight_grads/pallas_call | solution.py:289
  80.1 3.8 %token_outputs.1 = (bf16[2,768,1024]{2,1,0:T(8,128)(2,1)}, bf16[2,768,1024]{2,1,0:T(8,128)(2,1)}) custom-call(bf16[2,128,768]{2,1,0:T(8,128)(2,1)S(1)} %get-tuple-element.45.mix_ref, bf16[2,256,768]{2,1,0:T(8,128)(2,1)S(1)} %get-tuple-element.70.weights_ref, bf16[2,64,1024]{2,1,0:T(8,128)(2,1)S(1)} %get-tuple-element.71.own_outs_ref, ...), custom_call_target="tpu_custom_call" | custom-call | flops 1207959552 | bytes 9437184 | tf_op jit(solution)/shard_map/token_outputs/pallas_call | solution.py:454
  83.9 4.7 %all-to-all-done.4 = bf16[128,8,128]{2,1,0:T(8,128)(2,1)S(1)} async-done(((bf16[128,8,128]{2,1,0:T(8,128)(2,1)}), bf16[128,8,128]{2,1,0:T(8,128)(2,1)S(1)}, u32[]{:S(2)}, u32[]{:S(2)}) %all-to-all-start.4) | async-done | bytes 262176 | tf_op jit(solution)/shard_map/all_to_all | solution.py:485
  88.6 0.7 add_up.1
Async XLA Ops:
  4.7 3.1 %collective-permute-start = (bf16[8,8,4224]{2,1,0:T(8,128)(2,1)S(1)}, bf16[8,8,4224]{2,1,0:T(8,128)(2,1)S(1)}, u32[]{:S(2)}, u32[]{:S(2)}) collective-permute-start(bf16[8,8,4224]{2,1,0:T(8,128)(2,1)S(1)} %get-tuple-element.48), channel_id=1, source_target_pairs={{0,1},{1,0},{2,3},{3,2},{4,5},{5,4},{6,7},{7,6},{8,9},{9,8},{10,11... | collective-permute-start | bytes 1622024 | tf_op jit(solution)/shard_map/ppermute | solution.py:489
  7.6 33.4 %copy-start = (bf16[2,1024,512]{2,1,0:T(8,128)(2,1)S(1)}, bf16[2,1024,512]{2,1,0:T(8,128)(2,1)}, u32[]{:S(2)}) copy-start(bf16[2,1024,512]{2,1,0:T(8,128)(2,1)} %w_in_ref.1) | copy-start | bytes 6291460
  65.1 6.1 %collective-permute-start.1 = (bf16[8,8,4224]{2,1,0:T(8,128)(2,1)S(1)}, bf16[8,8,4224]{2,1,0:T(8,128)(2,1)S(1)}, u32[]{:S(2)}, u32[]{:S(2)}) collective-permute-start(bf16[8,8,4224]{2,1,0:T(8,128)(2,1)S(1)} %all_to_all.28.slots_ref), channel_id=1, source_target_pairs={{0,1},{1,0},{2,3},{3,2},{4,5},{5,4},{6,7},{7,6},{8,9},{9,8},{10,11... | collective-permute-start | bytes 1622024 | tf_op jit(solution)/shard_map/ppermute | solution.py:489
  73.8 14.8 %all-to-all-start.4 = ((bf16[128,8,128]{2,1,0:T(8,128)(2,1)}), bf16[128,8,128]{2,1,0:T(8,128)(2,1)S(1)}, u32[]{:S(2)}, u32[]{:S(2)}) async-start(bf16[128,8,128]{2,1,0:T(8,128)(2,1)} %bitcast), calls=%async_computation.4 | async-start | bytes 524288 | tf_op jit(solution)/shard_map/all_to_all | solution.py:485
